TPU v7x, 256 devices: a whole 4x4x8 slice. The times are simulated.
256 devices in a mesh: filt: 32 (over y, z_hi, core), space: 8 (over z_lo, x).
Axes of the slice: x: 4, y: 4, z: 8 (z_hi: 4, z_lo: 2; z = z_hi * 2 + z_lo), core: 2. Of those that a mesh axis runs over, the one named last changes fastest.
Arguments:
- volume: bfloat16 [256, 32, 4, 128], P('filt', 'space'), may hold values from -6 to 6
- kernel: bfloat16 [512, 3, 3, 3, 256], P('filt'), may hold values from -0.078125 to 0.078125
- filter_bias: bfloat16 [512], P('filt'), may hold values from -3 to 3
Outputs:
- pooled: bfloat16 [512, 16, 2, 64], P('filt', 'space')
All inputs are finite; a program needn't handle non-finite values.
Results may differ from a plain program's by a relative error of at most 0.001.
Values may be sent and summed in bfloat16 or wider, within the bound.
A program may use at most 64 MiB of HBM per device.

v0:
```python
import jax
import jax.numpy as jnp
from jax import lax
from jax.sharding import PartitionSpec as P

slope = 0.3


def with_halo(block, sides, width):
    for axis, dim in sides:
        count = lax.axis_size(axis)
        forward = [(i, i + 1) for i in range(count - 1)]
        backward = [(target, source) for source, target in forward]
        low = lax.ppermute(
            lax.slice_in_dim(block, block.shape[dim] - width, None, axis=dim), axis, forward
        )
        high = lax.ppermute(lax.slice_in_dim(block, 0, width, axis=dim), axis, backward)
        block = jnp.concatenate([low, block, high], axis=dim)
    return block


def convolve(inputs, weights, padding):
    return lax.conv_general_dilated(
        inputs[None],
        weights,
        (1, 1, 1),
        padding,
        dimension_numbers=("NCDHW", "ODHWI", "NCDHW"),
        preferred_element_type=jnp.float32,
    )[0]


def finish(summed, filter_bias):
    activated = summed + filter_bias.astype(jnp.float32)[:, None, None, None]
    activated = jnp.where(activated > 0, activated, slope * activated)
    filters, depth, height, across = activated.shape
    blocked = activated.reshape(filters, depth // 2, 2, height // 2, 2, across // 2, 2)
    return jnp.max(blocked, axis=(2, 4, 6)).astype(jnp.bfloat16)


def on_device(volume, kernel, filter_bias):
    local_in, slab_depth, height, across = volume.shape
    padded = with_halo(volume, (("space", 1),), 1)
    zeroed = jnp.zeros((kernel.shape[0], slab_depth, height, across), jnp.float32)
    summed = zeroed + convolve(
        lax.all_gather(padded, "filt", axis=0, tiled=True), kernel, ((0, 0), (1, 1), (1, 1))
    )
    return finish(summed, filter_bias)


def solution(mesh):
    in_specs = (P("filt", "space", None, None), P("filt", None, None, None, None), P("filt"))
    out_specs = P("filt", "space", None, None)
    return jax.shard_map(
        on_device, mesh=mesh, in_specs=in_specs, out_specs=out_specs, check_vma=False
    )
```

profile of v0, /device:TPU:7, one launch (start us, length us, event | category | flops | bytes accessed | tf_op | source)
XLA Modules:
  0.0 98.8 jit_solution(1009742245548532842)
XLA Ops:
  6.5 0.0 copy-start
  6.5 0.0 all-gather.2.cloned.1.call-start
  6.5 0.8 fusion.16
  7.3 3.5 %collective-permute-start = (bf16[8,1,4,128]{3,2,1,0:T(4,128)(2,1)S(1)}, bf16[8,1,4,128]{3,2,1,0:T(4,128)(2,1)S(1)}, u32[]{:S(2)}, u32[]{:S(2)}) collective-permute-start(bf16[8,1,4,128]{3,2,1,0:T(4,128)(2,1)S(1)} %get-tuple-element.5), channel_id=1, source_target_pairs={{0,1},{1,2},{2,3},{3,4},{4,5},{5,6},{6,7},{8,9},{9,10},{10,11},{11... | collective-permute-start | bytes 24584 | tf_op jit(solution)/shard_map/ppermute | solution.py:14
  10.8 1.9 %collective-permute-start.1 = (bf16[8,1,4,128]{3,2,1,0:T(4,128)(2,1)S(1)}, bf16[8,1,4,128]{3,2,1,0:T(4,128)(2,1)S(1)}, u32[]{:S(2)}, u32[]{:S(2)}) collective-permute-start(bf16[8,1,4,128]{3,2,1,0:T(4,128)(2,1)S(1)} %get-tuple-element.6), channel_id=1, source_target_pairs={{1,0},{2,1},{3,2},{4,3},{5,4},{6,5},{7,6},{9,8},{10,9},{11,10},{12... | collective-permute-start | bytes 24584 | tf_op jit(solution)/shard_map/ppermute | solution.py:17
  12.7 0.0 collective-permute-done
  12.7 4.6 %collective-permute-done.1 = bf16[8,1,4,128]{3,2,1,0:T(4,128)(2,1)S(1)} collective-permute-done((bf16[8,1,4,128]{3,2,1,0:T(4,128)(2,1)S(1)}, bf16[8,1,4,128]{3,2,1,0:T(4,128)(2,1)S(1)}, u32[]{:S(2)}, u32[]{:S(2)}) %collective-permute-start.1) | collective-permute-done | bytes 8224 | tf_op jit(solution)/shard_map/ppermute | solution.py:17
  17.3 1.4 %pad_maximum_fusion = bf16[8,6,4,128]{3,2,1,0:T(4,128)(2,1)} fusion(bf16[8,1,4,128]{3,2,1,0:T(4,128)(2,1)S(1)} %collective-permute-done.1, bf16[8,4,4,128]{3,2,1,0:T(4,128)(2,1)} %param.3, bf16[8,1,4,128]{3,2,1,0:T(4,128)(2,1)S(1)} %collective-permute-done), kind=kLoop, calls=%fused_computation.13 | loop fusion | flops 49152 | bytes 98304 | tf_op jit(solution)/shard_map/concatenate | solution.py:18
  18.7 0.0 all-gather.2.cloned.1.call-update
  18.7 0.7 convert_element_type.6
  19.4 56.3 %all-gather.2.cloned.1.call-done = bf16[256,6,4,128]{3,2,1,0:T(4,128)(2,1)} async-done(((bf16[8,6,4,128]{3,2,1,0:T(4,128)(2,1)}), bf16[256,6,4,128]{3,2,1,0:T(4,128)(2,1)}) %all-gather.2.cloned.1.call-update) | async-done | bytes 1572880 | tf_op jit(solution)/shard_map/all_gather | solution.py:46
  75.6 3.2 %copy.26 = bf16[256,6,4,1,128]{0,2,4,1,3:T(4,128)(2,1)S(1)} copy(bf16[256,6,4,1,128]{4,2,1,0,3:T(4,128)(2,1)} %bitcast.17) | data formatting | bytes 3145728
  78.9 0.6 pad.clone
  79.5 0.0 copy-start.1
  79.5 0.2 copy.21
  79.8 0.0 copy-done
  79.8 0.4 copy-done.1
  80.2 8.4 %fusion.8 = f32[4,4,8,17,16]{4,2,3,1,0:T(8,128)S(1)} fusion(bf16[16,3,3,3,256]{4,0,3,2,1:T(8,128)(2,1)S(1)} %copy-done, bf16[256,6,4,1,7,2]{0,4,5,2,1,3:T(8,128)(2,1)S(1)} %slice.10, bf16[256,6,4,1,8,17]{0,4,5,2,1,3:T(8,128)(2,1)S(1)} %copy.21, pred[8,17]{0,1:T(8,128)(4,1)S(1)} %copy-done.1), kind=kOutput, calls=%fused_computation.9 | convolution fusion | flops 406718464 | bytes 2203784 | tf_op jit(solution)/shard_map/conv_general_dilated | solution.py:23
  88.6 0.8 copy.22
  89.4 0.3 reshape.9
  89.8 0.3 copy.23
  90.1 1.2 %fusion.11 = bf16[16,2,2,64]{0,3,2,1:T(8,128)(2,1)S(1)} fusion(f32[16,2,2,2,2,64,2]{0,6,5,4,3,2,1:T(2,128)S(1)} %bitcast.16, f32[16]{0:T(128)S(1)} %convert_element_type.6), kind=kLoop, calls=%fused_computation.10 | loop fusion | flops 159744 | bytes 139328 | tf_op jit(solution)/shard_map/reduce_max | solution.py:38
  91.3 0.1 copy.24
  91.4 0.6 copy.25
  (2 shorter events, 0.1 us)
Async XLA Ops:
  6.5 73.3 %copy-start = (bf16[16,3,3,3,256]{4,0,3,2,1:T(8,128)(2,1)S(1)}, bf16[16,3,3,3,256]{4,0,3,2,1:T(8,128)(2,1)}, u32[]{:S(2)}) copy-start(bf16[16,3,3,3,256]{4,0,3,2,1:T(8,128)(2,1)} %param.4) | copy-start | bytes 663556
  6.5 69.1 %all-gather.2.cloned.1.call-start = ((), (), s32[]{:S(2)}) async-start(), calls=%async_computation | async-start | bytes 1622016 | tf_op jit(solution)/shard_map/all_gather | solution.py:46
  7.3 5.4 %collective-permute-start = (bf16[8,1,4,128]{3,2,1,0:T(4,128)(2,1)S(1)}, bf16[8,1,4,128]{3,2,1,0:T(4,128)(2,1)S(1)}, u32[]{:S(2)}, u32[]{:S(2)}) collective-permute-start(bf16[8,1,4,128]{3,2,1,0:T(4,128)(2,1)S(1)} %get-tuple-element.5), channel_id=1, source_target_pairs={{0,1},{1,2},{2,3},{3,4},{4,5},{5,6},{6,7},{8,9},{9,10},{10,11},{11... | collective-permute-start | bytes 24584 | tf_op jit(solution)/shard_map/ppermute | solution.py:14
  10.8 6.5 %collective-permute-start.1 = (bf16[8,1,4,128]{3,2,1,0:T(4,128)(2,1)S(1)}, bf16[8,1,4,128]{3,2,1,0:T(4,128)(2,1)S(1)}, u32[]{:S(2)}, u32[]{:S(2)}) collective-permute-start(bf16[8,1,4,128]{3,2,1,0:T(4,128)(2,1)S(1)} %get-tuple-element.6), channel_id=1, source_target_pairs={{1,0},{2,1},{3,2},{4,3},{5,4},{6,5},{7,6},{9,8},{10,9},{11,10},{12... | collective-permute-start | bytes 24584 | tf_op jit(solution)/shard_map/ppermute | solution.py:17
  79.5 0.7 copy-start.1
Sparse Core Ops, SparseCore 0:
  18.8 56.7 all-gather.1
where the time goes:
time: 100 us; the launch traced here: 98.8 us
  waiting for transfers between devices  60.9 us (61%)
  between operations  13.5 us (14%)
  matrix products  8.38 us (8%)
  local copies, waits for them, and re-layouts  7.48 us (7%)
  starting transfers between devices  5.37 us (5%)
  other arithmetic  3.25 us (3%)
    all_gather x1, waiting for transfers between devices, on_device(): lax.all_gather(padded, 'filt', axis=0, tiled=True)  56.3 us
    conv_general_dilated x1, matrix products, convolve(): lax.conv_general_dilated(inputs[None], weights, (1, 1, 1), padding, dimen...  8.38 us
    ppermute x1, waiting for transfers between devices, with_halo(): lax.ppermute(lax.slice_in_dim(block, 0, width, axis=dim), axis, backward)  4.57 us
    unnamed x5, local copies, waits for them, and re-layouts  3.63 us
    ppermute x1, starting transfers between devices, with_halo(): lax.ppermute(lax.slice_in_dim(block, block.shape[dim] - width, None, axis...  3.45 us
  transfers between devices with their start and end apart: 3, of which 2 were waited for; matrix products, arithmetic and copies ran while one was open for 1% of the time, Pallas kernels for 0%

commit v1 on v0

--- a/solution.py
+++ b/solution.py
@@ -1,9 +1,14 @@
+import functools
+
 import jax
 import jax.numpy as jnp
 from jax import lax
+from jax.experimental import pallas as pl
+from jax.experimental.pallas import tpu as pltpu
 from jax.sharding import PartitionSpec as P
 
 slope = 0.3
+MESH = pl.DeviceIdType.MESH
 
 
 def with_halo(block, sides, width):
@@ -17,6 +22,61 @@
         high = lax.ppermute(lax.slice_in_dim(block, 0, width, axis=dim), axis, backward)
         block = jnp.concatenate([low, block, high], axis=dim)
     return block
+
+
+def gather_kernel(n, x_ref, out_ref, local_sem, send_sem, recv_sem):
+    me = lax.axis_index("filt")
+    sp = lax.axis_index("space")
+    barrier = pltpu.get_barrier_semaphore()
+    for k in range(1, n):
+        peer = lax.rem(me + k, n)
+        pl.semaphore_signal(barrier, inc=1, device_id=(peer, sp), device_id_type=MESH)
+    pl.semaphore_wait(barrier, n - 1)
+
+    local = pltpu.make_async_copy(x_ref, out_ref.at[me], local_sem.at[0])
+    local.start()
+    copies = []
+    for k in range(1, n):
+        peer = lax.rem(me + k, n)
+        copy = pltpu.make_async_remote_copy(
+            src_ref=x_ref,
+            dst_ref=out_ref.at[me],
+            send_sem=send_sem.at[k],
+            recv_sem=recv_sem.at[me],
+            device_id=(peer, sp),
+            device_id_type=MESH,
+        )
+        copy.start()
+        copies.append(copy)
+    for k in range(1, n):
+        copies[k - 1].wait_send()
+    for k in range(1, n):
+        src = lax.rem(me + n - k, n)
+        pltpu.make_async_remote_copy(
+            src_ref=x_ref,
+            dst_ref=out_ref.at[src],
+            send_sem=send_sem.at[k],
+            recv_sem=recv_sem.at[src],
+            device_id=(src, sp),
+            device_id_type=MESH,
+        ).wait_recv()
+    local.wait()
+
+
+def gather_filt(block):
+    n = lax.axis_size("filt")
+    return pl.pallas_call(
+        functools.partial(gather_kernel, n),
+        out_shape=jax.ShapeDtypeStruct((n,) + block.shape, block.dtype),
+        in_specs=[pl.BlockSpec(memory_space=pl.ANY)],
+        out_specs=pl.BlockSpec(memory_space=pl.ANY),
+        scratch_shapes=[
+            pltpu.SemaphoreType.DMA((1,)),
+            pltpu.SemaphoreType.DMA((n,)),
+            pltpu.SemaphoreType.DMA((n,)),
+        ],
+        compiler_params=pltpu.CompilerParams(collective_id=0, has_side_effects=True),
+    )(block)
 
 
 def convolve(inputs, weights, padding):
@@ -39,12 +99,10 @@
 
 
 def on_device(volume, kernel, filter_bias):
-    local_in, slab_depth, height, across = volume.shape
     padded = with_halo(volume, (("space", 1),), 1)
-    zeroed = jnp.zeros((kernel.shape[0], slab_depth, height, across), jnp.float32)
-    summed = zeroed + convolve(
-        lax.all_gather(padded, "filt", axis=0, tiled=True), kernel, ((0, 0), (1, 1), (1, 1))
-    )
+    gathered = gather_filt(padded)
+    gathered = gathered.reshape((-1,) + gathered.shape[2:])
+    summed = convolve(gathered, kernel, ((0, 0), (1, 1), (1, 1)))
     return finish(summed, filter_bias)
 
 

time: 100 us -> 75.9 us (0.76)
  waiting for transfers between devices: 60.9 us -> 3.92 us
  Pallas kernels: 0 us -> 47.1 us
  between operations: 13.5 us -> 0.1 us
    all_gather x1 -> x0, waiting for transfers between devices: 56.3 us -> none  [on_device(): lax.all_gather(padded, 'filt', axis=0, tiled=True)]
    pallas_call x0 -> x1, Pallas kernels: none -> 47.1 us  [gather_filt(): pl.pallas_call(functools.partial(gather_kernel, n), out_shape=jax.ShapeDt...]
    another operation x0 -> x2, local copies, waits for them, and re-layouts: none -> 3.88 us  [convolve(): inputs[None]]
    unnamed x5 -> x4, local copies, waits for them, and re-layouts: 3.63 us -> 0.39 us
  transfers between devices with their start and end apart: 3 -> 2, of which waited for: 2 -> 1; matrix products, arithmetic and copies ran while one was open for 1% -> 1% of each run, Pallas kernels for 0% -> 0%
where the time goes in v1:
time: 75.9 us; the launch traced here: 75.7 us
  Pallas kernels  47.1 us (62%)
  matrix products  8.38 us (11%)
  local copies, waits for them, and re-layouts  7.5 us (10%)
  starting transfers between devices  5.37 us (7%)
  waiting for transfers between devices  3.92 us (5%)
  other arithmetic  3.24 us (4%)
    pallas_call x1, Pallas kernels, gather_filt(): pl.pallas_call(functools.partial(gather_kernel, n), out_shape=jax.ShapeDt...  47.1 us
    conv_general_dilated x1, matrix products, convolve(): lax.conv_general_dilated(inputs[None], weights, (1, 1, 1), padding, dimen...  8.38 us
    ppermute x1, waiting for transfers between devices, with_halo(): lax.ppermute(lax.slice_in_dim(block, 0, width, axis=dim), axis, backward)  3.91 us
    another operation x2, local copies, waits for them, and re-layouts, convolve(): inputs[None]  3.88 us
    ppermute x1, starting transfers between devices, with_halo(): lax.ppermute(lax.slice_in_dim(block, block.shape[dim] - width, None, axis...  3.45 us
    ppermute x1, starting transfers between devices, with_halo(): lax.ppermute(lax.slice_in_dim(block, 0, width, axis=dim), axis, backward)  1.92 us
    conv_general_dilated x6, local copies, waits for them, and re-layouts, convolve(): lax.conv_general_dilated(inputs[None], weights, (1, 1, 1), padding, dimen...  1.75 us
  transfers between devices with their start and end apart: 2, of which 1 were waited for; matrix products, arithmetic and copies ran while one was open for 1% of the time, Pallas kernels for 0%

profile of v1, /device:TPU:7, one launch (start us, length us, event | category | flops | bytes accessed | tf_op | source)
XLA Modules:
  0.0 75.7 jit_solution(14717567104722641509)
XLA Ops:
  0.0 0.0 copy-start
  0.0 0.8 %fusion.16 = (bf16[8,1,4,128]{3,2,1,0:T(4,128)(2,1)S(1)}, bf16[8,1,4,128]{3,2,1,0:T(4,128)(2,1)S(1)}) fusion(bf16[8,4,4,128]{3,2,1,0:T(4,128)(2,1)} %param.3), kind=kLoop, calls=%fused_computation.17 | loop fusion | bytes 32768 | tf_op jit(solution)/shard_map/slice | solution.py:20
  0.8 3.5 %collective-permute-start = (bf16[8,1,4,128]{3,2,1,0:T(4,128)(2,1)S(1)}, bf16[8,1,4,128]{3,2,1,0:T(4,128)(2,1)S(1)}, u32[]{:S(2)}, u32[]{:S(2)}) collective-permute-start(bf16[8,1,4,128]{3,2,1,0:T(4,128)(2,1)S(1)} %get-tuple-element.5), channel_id=1, source_target_pairs={{0,1},{1,2},{2,3},{3,4},{4,5},{5,6},{6,7},{8,9},{9,10},{10,11},{11... | collective-permute-start | bytes 24584 | tf_op jit(solution)/shard_map/ppermute | solution.py:19
  4.2 1.9 %collective-permute-start.1 = (bf16[8,1,4,128]{3,2,1,0:T(4,128)(2,1)S(1)}, bf16[8,1,4,128]{3,2,1,0:T(4,128)(2,1)S(1)}, u32[]{:S(2)}, u32[]{:S(2)}) collective-permute-start(bf16[8,1,4,128]{3,2,1,0:T(4,128)(2,1)S(1)} %get-tuple-element.6), channel_id=1, source_target_pairs={{1,0},{2,1},{3,2},{4,3},{5,4},{6,5},{7,6},{9,8},{10,9},{11,10},{12... | collective-permute-start | bytes 24584 | tf_op jit(solution)/shard_map/ppermute | solution.py:22
  6.2 0.7 convert_element_type.6
  6.8 0.0 collective-permute-done
  6.8 3.9 %collective-permute-done.1 = bf16[8,1,4,128]{3,2,1,0:T(4,128)(2,1)S(1)} collective-permute-done((bf16[8,1,4,128]{3,2,1,0:T(4,128)(2,1)S(1)}, bf16[8,1,4,128]{3,2,1,0:T(4,128)(2,1)S(1)}, u32[]{:S(2)}, u32[]{:S(2)}) %collective-permute-start.1) | collective-permute-done | bytes 8224 | tf_op jit(solution)/shard_map/ppermute | solution.py:22
  10.7 1.4 %pad_maximum_fusion.x_ref = bf16[8,6,4,128]{3,2,1,0:T(4,128)(2,1)} fusion(bf16[8,1,4,128]{3,2,1,0:T(4,128)(2,1)S(1)} %collective-permute-done.1, bf16[8,4,4,128]{3,2,1,0:T(4,128)(2,1)} %param.3, bf16[8,1,4,128]{3,2,1,0:T(4,128)(2,1)S(1)} %collective-permute-done), kind=kLoop, calls=%fused_computation.13 | loop fusion | flops 49152 | bytes 98304 | tf_op jit(solution)/shard_map/concatenate | solution.py:23
  12.1 47.1 %shard_map.37 = bf16[32,8,6,4,128]{4,3,2,1,0:T(4,128)(2,1)} custom-call(bf16[8,6,4,128]{3,2,1,0:T(4,128)(2,1)} %pad_maximum_fusion.x_ref), custom_call_target="tpu_custom_call" | custom-call | tf_op jit(solution)/shard_map/pallas_call | solution.py:68
  59.3 3.2 %copy.19 = bf16[256,6,4,1,128]{0,2,4,1,3:T(4,128)(2,1)S(1)} copy(bf16[256,6,4,1,128]{4,2,1,0,3:T(4,128)(2,1)} %bitcast.16) | data formatting | bytes 3145728 | tf_op jit(solution)/shard_map/broadcast_in_dim;reshape | solution.py:84
  62.5 0.6 pad
  63.2 0.0 copy-start.1
  63.2 0.2 copy.21
  63.5 0.0 copy-done
  63.5 0.4 copy-done.1
  63.9 8.4 %fusion.8 = f32[4,4,8,17,16]{4,2,3,1,0:T(8,128)S(1)} fusion(bf16[16,3,3,3,256]{4,0,3,2,1:T(8,128)(2,1)S(1)} %copy-done, bf16[256,6,4,1,7,2]{0,4,5,2,1,3:T(8,128)(2,1)S(1)} %slice.10, bf16[256,6,4,1,8,17]{0,4,5,2,1,3:T(8,128)(2,1)S(1)} %copy.21, pred[8,17]{0,1:T(8,128)(4,1)S(1)} %copy-done.1), kind=kOutput, calls=%fused_computation.9 | convolution fusion | flops 406718464 | bytes 2203784 | tf_op jit(solution)/shard_map/conv_general_dilated | solution.py:83
  72.3 0.8 %copy.22 = f32[4,4,8,17,16]{3,2,4,1,0:T(8,128)S(1)} copy(f32[4,4,8,17,16]{4,2,3,1,0:T(8,128)S(1)} %fusion.8) | data formatting | bytes 278528 | tf_op jit(solution)/shard_map/conv_general_dilated | solution.py:83
  73.1 0.3 reshape.9
  73.4 0.3 copy.23
  73.8 1.2 %fusion.11 = bf16[16,2,2,64]{0,3,2,1:T(8,128)(2,1)S(1)} fusion(f32[16,2,2,2,2,64,2]{0,6,5,4,3,2,1:T(2,128)S(1)} %bitcast.17, f32[16]{0:T(128)S(1)} %convert_element_type.6), kind=kLoop, calls=%fused_computation.10 | loop fusion | flops 159744 | bytes 139328 | tf_op jit(solution)/shard_map/reduce_max | solution.py:98
  74.9 0.1 copy.24
  75.0 0.6 copy.25
  (2 shorter events, 0.1 us)
Async XLA Ops:
  0.0 63.5 %copy-start = (bf16[16,3,3,3,256]{4,0,3,2,1:T(8,128)(2,1)S(1)}, bf16[16,3,3,3,256]{4,0,3,2,1:T(8,128)(2,1)}, u32[]{:S(2)}) copy-start(bf16[16,3,3,3,256]{4,0,3,2,1:T(8,128)(2,1)} %param.4) | copy-start | bytes 663556
  0.8 6.1 %collective-permute-start = (bf16[8,1,4,128]{3,2,1,0:T(4,128)(2,1)S(1)}, bf16[8,1,4,128]{3,2,1,0:T(4,128)(2,1)S(1)}, u32[]{:S(2)}, u32[]{:S(2)}) collective-permute-start(bf16[8,1,4,128]{3,2,1,0:T(4,128)(2,1)S(1)} %get-tuple-element.5), channel_id=1, source_target_pairs={{0,1},{1,2},{2,3},{3,4},{4,5},{5,6},{6,7},{8,9},{9,10},{10,11},{11... | collective-permute-start | bytes 24584 | tf_op jit(solution)/shard_map/ppermute | solution.py:19
  4.2 6.5 %collective-permute-start.1 = (bf16[8,1,4,128]{3,2,1,0:T(4,128)(2,1)S(1)}, bf16[8,1,4,128]{3,2,1,0:T(4,128)(2,1)S(1)}, u32[]{:S(2)}, u32[]{:S(2)}) collective-permute-start(bf16[8,1,4,128]{3,2,1,0:T(4,128)(2,1)S(1)} %get-tuple-element.6), channel_id=1, source_target_pairs={{1,0},{2,1},{3,2},{4,3},{5,4},{6,5},{7,6},{9,8},{10,9},{11,10},{12... | collective-permute-start | bytes 24584 | tf_op jit(solution)/shard_map/ppermute | solution.py:22
  63.2 0.7 copy-start.1

commit v2 on v1

--- a/solution.py
+++ b/solution.py
@@ -24,42 +24,50 @@
     return block
 
 
-def gather_kernel(n, x_ref, out_ref, local_sem, send_sem, recv_sem):
+def gather_kernel(n, x_ref, out_ref, local_sem, send_sem, fwd_sem, recv_sem):
     me = lax.axis_index("filt")
     sp = lax.axis_index("space")
+    chips = n // 2
+    core = lax.rem(me, 2)
+    chip = me // 2
+    sib = me + 1 - 2 * core
+    peers = [lax.rem(chip + k, chips) * 2 + core for k in range(1, chips)]
+    sources = [lax.rem(chip + chips - k, chips) * 2 + core for k in range(1, chips)]
+
     barrier = pltpu.get_barrier_semaphore()
-    for k in range(1, n):
-        peer = lax.rem(me + k, n)
+    for peer in [sib] + peers:
         pl.semaphore_signal(barrier, inc=1, device_id=(peer, sp), device_id_type=MESH)
-    pl.semaphore_wait(barrier, n - 1)
+    pl.semaphore_wait(barrier, chips)
+
+    def remote(src, dst_slot, sem, dev):
+        return pltpu.make_async_remote_copy(
+            src_ref=src,
+            dst_ref=out_ref.at[dst_slot],
+            send_sem=sem,
+            recv_sem=recv_sem.at[dst_slot],
+            device_id=(dev, sp),
+            device_id_type=MESH,
+        )
 
     local = pltpu.make_async_copy(x_ref, out_ref.at[me], local_sem.at[0])
     local.start()
-    copies = []
-    for k in range(1, n):
-        peer = lax.rem(me + k, n)
-        copy = pltpu.make_async_remote_copy(
-            src_ref=x_ref,
-            dst_ref=out_ref.at[me],
-            send_sem=send_sem.at[k],
-            recv_sem=recv_sem.at[me],
-            device_id=(peer, sp),
-            device_id_type=MESH,
-        )
+    sends = [remote(x_ref, me, send_sem.at[0], sib)]
+    for k, peer in enumerate(peers):
+        sends.append(remote(x_ref, me, send_sem.at[k + 1], peer))
+    for copy in sends:
         copy.start()
-        copies.append(copy)
-    for k in range(1, n):
-        copies[k - 1].wait_send()
-    for k in range(1, n):
-        src = lax.rem(me + n - k, n)
-        pltpu.make_async_remote_copy(
-            src_ref=x_ref,
-            dst_ref=out_ref.at[src],
-            send_sem=send_sem.at[k],
-            recv_sem=recv_sem.at[src],
-            device_id=(src, sp),
-            device_id_type=MESH,
-        ).wait_recv()
+    forwards = []
+    for k, src in enumerate(sources):
+        remote(out_ref.at[src], src, fwd_sem.at[k], src).wait_recv()
+        copy = remote(out_ref.at[src], src, fwd_sem.at[k], sib)
+        copy.start()
+        forwards.append(copy)
+    remote(out_ref.at[sib], sib, send_sem.at[0], sib).wait_recv()
+    for k in range(1, chips):
+        src = lax.rem(chip + chips - k, chips) * 2 + 1 - core
+        remote(out_ref.at[src], src, fwd_sem.at[k - 1], sib).wait_recv()
+    for copy in sends + forwards:
+        copy.wait_send()
     local.wait()
 
 
@@ -72,7 +80,8 @@
         out_specs=pl.BlockSpec(memory_space=pl.ANY),
         scratch_shapes=[
             pltpu.SemaphoreType.DMA((1,)),
-            pltpu.SemaphoreType.DMA((n,)),
+            pltpu.SemaphoreType.DMA((n // 2,)),
+            pltpu.SemaphoreType.DMA((n // 2,)),
             pltpu.SemaphoreType.DMA((n,)),
         ],
         compiler_params=pltpu.CompilerParams(collective_id=0, has_side_effects=True),

time: 75.9 us -> 58.1 us (0.77)
  Pallas kernels: 47.1 us -> 29.3 us
    pallas_call x1, Pallas kernels: 47.1 us -> 29.3 us  [gather_filt(): pl.pallas_call(functools.partial(gather_kernel, n), out_shape=jax.ShapeDt...]
where the time goes in v2:
time: 58.1 us; the launch traced here: 57.8 us
  Pallas kernels  29.3 us (50%)
  matrix products  8.36 us (14%)
  local copies, waits for them, and re-layouts  7.5 us (13%)
  starting transfers between devices  5.37 us (9%)
  waiting for transfers between devices  3.92 us (7%)
  other arithmetic  3.24 us (6%)
    pallas_call x1, Pallas kernels, gather_filt(): pl.pallas_call(functools.partial(gather_kernel, n), out_shape=jax.ShapeDt...  29.3 us
    conv_general_dilated x1, matrix products, convolve(): lax.conv_general_dilated(inputs[None], weights, (1, 1, 1), padding, dimen...  8.36 us
    ppermute x1, waiting for transfers between devices, with_halo(): lax.ppermute(lax.slice_in_dim(block, 0, width, axis=dim), axis, backward)  3.91 us
    another operation x2, local copies, waits for them, and re-layouts, convolve(): inputs[None]  3.88 us
    ppermute x1, starting transfers between devices, with_halo(): lax.ppermute(lax.slice_in_dim(block, block.shape[dim] - width, None, axis...  3.45 us
    ppermute x1, starting transfers between devices, with_halo(): lax.ppermute(lax.slice_in_dim(block, 0, width, axis=dim), axis, backward)  1.92 us
    conv_general_dilated x6, local copies, waits for them, and re-layouts, convolve(): lax.conv_general_dilated(inputs[None], weights, (1, 1, 1), padding, dimen...  1.75 us
    concatenate x1, other arithmetic, with_halo(): block = jnp.concatenate([low, block, high], axis=dim)  1.4 us
  transfers between devices with their start and end apart: 2, of which 1 were waited for; matrix products, arithmetic and copies ran while one was open for 1% of the time, Pallas kernels for 0%

profile of v2, /device:TPU:7, one launch (start us, length us, event | category | flops | bytes accessed | tf_op | source)
XLA Modules:
  0.0 57.8 jit_solution(4206470607816914219)
XLA Ops:
  0.0 0.0 copy-start
  0.0 0.8 %fusion.16 = (bf16[8,1,4,128]{3,2,1,0:T(4,128)(2,1)S(1)}, bf16[8,1,4,128]{3,2,1,0:T(4,128)(2,1)S(1)}) fusion(bf16[8,4,4,128]{3,2,1,0:T(4,128)(2,1)} %param.3), kind=kLoop, calls=%fused_computation.17 | loop fusion | bytes 32768 | tf_op jit(solution)/shard_map/slice | solution.py:20
  0.8 3.5 %collective-permute-start = (bf16[8,1,4,128]{3,2,1,0:T(4,128)(2,1)S(1)}, bf16[8,1,4,128]{3,2,1,0:T(4,128)(2,1)S(1)}, u32[]{:S(2)}, u32[]{:S(2)}) collective-permute-start(bf16[8,1,4,128]{3,2,1,0:T(4,128)(2,1)S(1)} %get-tuple-element.5), channel_id=1, source_target_pairs={{0,1},{1,2},{2,3},{3,4},{4,5},{5,6},{6,7},{8,9},{9,10},{10,11},{11... | collective-permute-start | bytes 24584 | tf_op jit(solution)/shard_map/ppermute | solution.py:19
  4.2 1.9 %collective-permute-start.1 = (bf16[8,1,4,128]{3,2,1,0:T(4,128)(2,1)S(1)}, bf16[8,1,4,128]{3,2,1,0:T(4,128)(2,1)S(1)}, u32[]{:S(2)}, u32[]{:S(2)}) collective-permute-start(bf16[8,1,4,128]{3,2,1,0:T(4,128)(2,1)S(1)} %get-tuple-element.6), channel_id=1, source_target_pairs={{1,0},{2,1},{3,2},{4,3},{5,4},{6,5},{7,6},{9,8},{10,9},{11,10},{12... | collective-permute-start | bytes 24584 | tf_op jit(solution)/shard_map/ppermute | solution.py:22
  6.2 0.7 %convert_element_type.6 = f32[16]{0:T(128)S(1)} convert(bf16[16]{0:T(256)(128)(2,1)} %param.5) | non-fusion elementwise | flops 16 | bytes 96 | tf_op jit(solution)/shard_map/convert_element_type | solution.py:103
  6.8 0.0 collective-permute-done
  6.8 3.9 %collective-permute-done.1 = bf16[8,1,4,128]{3,2,1,0:T(4,128)(2,1)S(1)} collective-permute-done((bf16[8,1,4,128]{3,2,1,0:T(4,128)(2,1)S(1)}, bf16[8,1,4,128]{3,2,1,0:T(4,128)(2,1)S(1)}, u32[]{:S(2)}, u32[]{:S(2)}) %collective-permute-start.1) | collective-permute-done | bytes 8224 | tf_op jit(solution)/shard_map/ppermute | solution.py:22
  10.7 1.4 %pad_maximum_fusion.x_ref = bf16[8,6,4,128]{3,2,1,0:T(4,128)(2,1)} fusion(bf16[8,1,4,128]{3,2,1,0:T(4,128)(2,1)S(1)} %collective-permute-done.1, bf16[8,4,4,128]{3,2,1,0:T(4,128)(2,1)} %param.3, bf16[8,1,4,128]{3,2,1,0:T(4,128)(2,1)S(1)} %collective-permute-done), kind=kLoop, calls=%fused_computation.13 | loop fusion | flops 49152 | bytes 98304 | tf_op jit(solution)/shard_map/concatenate | solution.py:23
  12.1 29.3 %shard_map.37 = bf16[32,8,6,4,128]{4,3,2,1,0:T(4,128)(2,1)} custom-call(bf16[8,6,4,128]{3,2,1,0:T(4,128)(2,1)} %pad_maximum_fusion.x_ref), custom_call_target="tpu_custom_call" | custom-call | tf_op jit(solution)/shard_map/pallas_call | solution.py:76
  41.5 3.2 %copy.19 = bf16[256,6,4,1,128]{0,2,4,1,3:T(4,128)(2,1)S(1)} copy(bf16[256,6,4,1,128]{4,2,1,0,3:T(4,128)(2,1)} %bitcast.16) | data formatting | bytes 3145728 | tf_op jit(solution)/shard_map/broadcast_in_dim;reshape | solution.py:93
  44.7 0.6 %pad = bf16[256,6,4,1,136]{0,2,4,1,3:T(4,128)(2,1)S(1)} pad(bf16[256,6,4,1,128]{0,2,4,1,3:T(4,128)(2,1)S(1)} %copy.19, bf16[]{:T(256)} %constant.9), padding=0_0x0_0x0_0x0_0x1_7 | pad | bytes 3244034 | tf_op jit(solution)/shard_map/broadcast_in_dim;reshape | solution.py:93
  45.4 0.0 copy-start.1
  45.4 0.2 copy.21
  45.7 0.0 copy-done
  45.7 0.4 copy-done.1
  46.1 8.4 %fusion.8 = f32[4,4,8,17,16]{4,2,3,1,0:T(8,128)S(1)} fusion(bf16[16,3,3,3,256]{4,0,3,2,1:T(8,128)(2,1)S(1)} %copy-done, bf16[256,6,4,1,7,2]{0,4,5,2,1,3:T(8,128)(2,1)S(1)} %slice.10, bf16[256,6,4,1,8,17]{0,4,5,2,1,3:T(8,128)(2,1)S(1)} %copy.21, pred[8,17]{0,1:T(8,128)(4,1)S(1)} %copy-done.1), kind=kOutput, calls=%fused_computation.9 | convolution fusion | flops 406718464 | bytes 2203784 | tf_op jit(solution)/shard_map/conv_general_dilated | solution.py:92
  54.4 0.8 %copy.22 = f32[4,4,8,17,16]{3,2,4,1,0:T(8,128)S(1)} copy(f32[4,4,8,17,16]{4,2,3,1,0:T(8,128)S(1)} %fusion.8) | data formatting | bytes 278528 | tf_op jit(solution)/shard_map/conv_general_dilated | solution.py:92
  55.3 0.3 reshape.9
  55.6 0.3 copy.23
  55.9 1.2 %fusion.11 = bf16[16,2,2,64]{0,3,2,1:T(8,128)(2,1)S(1)} fusion(f32[16,2,2,2,2,64,2]{0,6,5,4,3,2,1:T(2,128)S(1)} %bitcast.17, f32[16]{0:T(128)S(1)} %convert_element_type.6), kind=kLoop, calls=%fused_computation.10 | loop fusion | flops 159744 | bytes 139328 | tf_op jit(solution)/shard_map/reduce_max | solution.py:107
  57.1 0.1 copy.24
  57.2 0.6 %copy.25 = bf16[16,2,2,64]{3,2,1,0:T(2,128)(2,1)} copy(bf16[16,2,2,64]{3,0,2,1:T(8,128)(2,1)S(1)} %copy.24) | data formatting | bytes 16384 | tf_op jit(solution)/shard_map/convert_element_type | solution.py:107
  (2 shorter events, 0.1 us)
Async XLA Ops:
  0.0 45.7 %copy-start = (bf16[16,3,3,3,256]{4,0,3,2,1:T(8,128)(2,1)S(1)}, bf16[16,3,3,3,256]{4,0,3,2,1:T(8,128)(2,1)}, u32[]{:S(2)}) copy-start(bf16[16,3,3,3,256]{4,0,3,2,1:T(8,128)(2,1)} %param.4) | copy-start | bytes 663556
  0.8 6.1 %collective-permute-start = (bf16[8,1,4,128]{3,2,1,0:T(4,128)(2,1)S(1)}, bf16[8,1,4,128]{3,2,1,0:T(4,128)(2,1)S(1)}, u32[]{:S(2)}, u32[]{:S(2)}) collective-permute-start(bf16[8,1,4,128]{3,2,1,0:T(4,128)(2,1)S(1)} %get-tuple-element.5), channel_id=1, source_target_pairs={{0,1},{1,2},{2,3},{3,4},{4,5},{5,6},{6,7},{8,9},{9,10},{10,11},{11... | collective-permute-start | bytes 24584 | tf_op jit(solution)/shard_map/ppermute | solution.py:19
  4.2 6.5 %collective-permute-start.1 = (bf16[8,1,4,128]{3,2,1,0:T(4,128)(2,1)S(1)}, bf16[8,1,4,128]{3,2,1,0:T(4,128)(2,1)S(1)}, u32[]{:S(2)}, u32[]{:S(2)}) collective-permute-start(bf16[8,1,4,128]{3,2,1,0:T(4,128)(2,1)S(1)} %get-tuple-element.6), channel_id=1, source_target_pairs={{1,0},{2,1},{3,2},{4,3},{5,4},{6,5},{7,6},{9,8},{10,9},{11,10},{12... | collective-permute-start | bytes 24584 | tf_op jit(solution)/shard_map/ppermute | solution.py:22
  45.4 0.7 %copy-start.1 = (pred[8,17]{0,1:T(8,128)(4,1)S(1)}, pred[8,17]{0,1:T(8,128)(4,1)}, u32[]{:S(2)}) copy-start(pred[8,17]{0,1:T(8,128)(4,1)} %constant.13) | copy-start | bytes 412

commit v3 on v2

--- a/solution.py
+++ b/solution.py
@@ -33,6 +33,10 @@
     sib = me + 1 - 2 * core
     peers = [lax.rem(chip + k, chips) * 2 + core for k in range(1, chips)]
     sources = [lax.rem(chip + chips - k, chips) * 2 + core for k in range(1, chips)]
+    rows = x_ref.shape[0]
+
+    def rows_of(slot):
+        return pl.ds(pl.multiple_of(slot * rows, rows), rows)
 
     barrier = pltpu.get_barrier_semaphore()
     for peer in [sib] + peers:
@@ -42,14 +46,14 @@
     def remote(src, dst_slot, sem, dev):
         return pltpu.make_async_remote_copy(
             src_ref=src,
-            dst_ref=out_ref.at[dst_slot],
+            dst_ref=out_ref.at[rows_of(dst_slot)],
             send_sem=sem,
             recv_sem=recv_sem.at[dst_slot],
             device_id=(dev, sp),
             device_id_type=MESH,
         )
 
-    local = pltpu.make_async_copy(x_ref, out_ref.at[me], local_sem.at[0])
+    local = pltpu.make_async_copy(x_ref, out_ref.at[rows_of(me)], local_sem.at[0])
     local.start()
     sends = [remote(x_ref, me, send_sem.at[0], sib)]
     for k, peer in enumerate(peers):
@@ -58,14 +62,14 @@
         copy.start()
     forwards = []
     for k, src in enumerate(sources):
-        remote(out_ref.at[src], src, fwd_sem.at[k], src).wait_recv()
-        copy = remote(out_ref.at[src], src, fwd_sem.at[k], sib)
+        remote(out_ref.at[rows_of(src)], src, fwd_sem.at[k], src).wait_recv()
+        copy = remote(out_ref.at[rows_of(src)], src, fwd_sem.at[k], sib)
         copy.start()
         forwards.append(copy)
-    remote(out_ref.at[sib], sib, send_sem.at[0], sib).wait_recv()
+    remote(out_ref.at[rows_of(sib)], sib, send_sem.at[0], sib).wait_recv()
     for k in range(1, chips):
         src = lax.rem(chip + chips - k, chips) * 2 + 1 - core
-        remote(out_ref.at[src], src, fwd_sem.at[k - 1], sib).wait_recv()
+        remote(out_ref.at[rows_of(src)], src, fwd_sem.at[k - 1], sib).wait_recv()
     for copy in sends + forwards:
         copy.wait_send()
     local.wait()
@@ -75,7 +79,7 @@
     n = lax.axis_size("filt")
     return pl.pallas_call(
         functools.partial(gather_kernel, n),
-        out_shape=jax.ShapeDtypeStruct((n,) + block.shape, block.dtype),
+        out_shape=jax.ShapeDtypeStruct((n * block.shape[0],) + block.shape[1:], block.dtype),
         in_specs=[pl.BlockSpec(memory_space=pl.ANY)],
         out_specs=pl.BlockSpec(memory_space=pl.ANY),
         scratch_shapes=[
@@ -88,31 +92,75 @@
     )(block)
 
 
-def convolve(inputs, weights, padding):
-    return lax.conv_general_dilated(
-        inputs[None],
-        weights,
-        (1, 1, 1),
-        padding,
-        dimension_numbers=("NCDHW", "ODHWI", "NCDHW"),
-        preferred_element_type=jnp.float32,
-    )[0]
+def conv_kernel(g_ref, w_ref, b_ref, o_ref, *, plane, row, depth):
+    g = g_ref[...]
+    cols = g.shape[1]
+    x = lax.broadcasted_iota(jnp.int32, g.shape, 1) % row
+    zero = jnp.zeros_like(g)
+    left = jnp.where(x == 0, zero, pltpu.roll(g, 1, 1))
+    right = jnp.where(x == row - 1, zero, pltpu.roll(g, cols - 1, 1))
+    stacked = jnp.concatenate([left, g, right], axis=0)
+    q = jnp.dot(w_ref[...], stacked, preferred_element_type=jnp.float32)
+    filters = o_ref.shape[0]
+    out_cols = depth * plane
+    acc = jnp.zeros((filters, out_cols), jnp.float32)
+    for a in range(3):
+        for b in range(3):
+            tap = q[(a * 3 + b) * filters:(a * 3 + b + 1) * filters]
+            shift = a * plane + (b - 1) * row
+            if b == 1:
+                acc = acc + tap[:, shift:shift + out_cols]
+                continue
+            pieces = []
+            for z in range(depth):
+                lo = z * plane + (row if b == 0 else 0)
+                hi = lo + plane - row
+                part = tap[:, lo + shift:hi + shift]
+                edge = jnp.zeros((filters, row), jnp.float32)
+                pieces += [edge, part] if b == 0 else [part, edge]
+            acc = acc + jnp.concatenate(pieces, axis=1)
+    pooled = []
+    for zp in range(depth // 2):
+        zmax = jnp.maximum(
+            acc[:, 2 * zp * plane:(2 * zp + 1) * plane],
+            acc[:, (2 * zp + 1) * plane:(2 * zp + 2) * plane],
+        )
+        for yp in range(plane // row // 2):
+            pooled.append(
+                jnp.maximum(
+                    zmax[:, 2 * yp * row:(2 * yp + 1) * row],
+                    zmax[:, (2 * yp + 1) * row:(2 * yp + 2) * row],
+                )
+            )
+    m = jnp.concatenate(pooled, axis=1)
+    m = jnp.maximum(m, pltpu.roll(m, m.shape[1] - 1, 1))
+    v = m + b_ref[...]
+    v = jnp.where(v > 0, v, slope * v).astype(jnp.bfloat16)
+    r = lax.broadcasted_iota(jnp.int32, (m.shape[1], m.shape[1] // 2), 0)
+    c = lax.broadcasted_iota(jnp.int32, (m.shape[1], m.shape[1] // 2), 1)
+    pick = (r == 2 * c).astype(jnp.bfloat16)
+    o_ref[...] = jnp.dot(v, pick, preferred_element_type=jnp.float32).astype(o_ref.dtype)
 
 
-def finish(summed, filter_bias):
-    activated = summed + filter_bias.astype(jnp.float32)[:, None, None, None]
-    activated = jnp.where(activated > 0, activated, slope * activated)
-    filters, depth, height, across = activated.shape
-    blocked = activated.reshape(filters, depth // 2, 2, height // 2, 2, across // 2, 2)
-    return jnp.max(blocked, axis=(2, 4, 6)).astype(jnp.bfloat16)
+def conv_pool(gathered, kernel, filter_bias, depth, height, across):
+    filters = kernel.shape[0]
+    weights = kernel.transpose(1, 2, 0, 3, 4).reshape(9 * filters, -1)
+    bias = filter_bias.astype(jnp.float32).reshape(filters, 1)
+    plane = height * across
+    out = pl.pallas_call(
+        functools.partial(conv_kernel, plane=plane, row=across, depth=depth),
+        out_shape=jax.ShapeDtypeStruct((filters, depth * plane // 8), jnp.bfloat16),
+        in_specs=[pl.BlockSpec(memory_space=pltpu.VMEM)] * 3,
+        out_specs=pl.BlockSpec(memory_space=pltpu.VMEM),
+    )(gathered, weights, bias)
+    return out.reshape(filters, depth // 2, height // 2, across // 2)
 
 
 def on_device(volume, kernel, filter_bias):
+    local_in, depth, height, across = volume.shape
     padded = with_halo(volume, (("space", 1),), 1)
-    gathered = gather_filt(padded)
-    gathered = gathered.reshape((-1,) + gathered.shape[2:])
-    summed = convolve(gathered, kernel, ((0, 0), (1, 1), (1, 1)))
-    return finish(summed, filter_bias)
+    gathered = gather_filt(padded.reshape(local_in, -1))
+    return conv_pool(gathered, kernel, filter_bias, depth, height, across)
 
 
 def solution(mesh):

time: 58.1 us -> 47.8 us (0.82)
  matrix products: 8.36 us -> 0 us
  Pallas kernels: 29.3 us -> 33.8 us
  waiting for transfers between devices: 3.92 us -> 1.42 us
  local copies, waits for them, and re-layouts: 7.5 us -> 5.24 us
  other arithmetic: 3.24 us -> 1.46 us
    conv_general_dilated x1 -> x0, matrix products: 8.36 us -> none  [convolve(): lax.conv_general_dilated(inputs[None], weights, (1, 1, 1), padding, dimen...]
    another operation x2 -> x0, local copies, waits for them, and re-layouts: 3.88 us -> none  [convolve(): inputs[None]]
    pallas_call x0 -> x1, Pallas kernels: none -> 3.56 us  [conv_pool(): pl.pallas_call(functools.partial(conv_kernel, plane=plane, row=across, de...]
    reshape x0 -> x3, local copies, waits for them, and re-layouts: none -> 2.71 us  [the longest x1 1.39 us: conv_pool(): return out.reshape(filters, depth // 2, height // 2, across // 2)]
    ppermute x1, waiting for transfers between devices: 3.91 us -> 1.42 us  [with_halo(): lax.ppermute(lax.slice_in_dim(block, 0, width, axis=dim), axis, backward)]
    conv_general_dilated x6 -> x0, local copies, waits for them, and re-layouts: 1.75 us -> none  [convolve(): lax.conv_general_dilated(inputs[None], weights, (1, 1, 1), padding, dimen...]
    reduce_max x1 -> x0, other arithmetic: 1.18 us -> none  [finish(): return jnp.max(blocked, axis=(2, 4, 6)).astype(jnp.bfloat16)]
    transpose x0 -> x1, local copies, waits for them, and re-layouts: none -> 1.09 us  [conv_pool(): weights = kernel.transpose(1, 2, 0, 3, 4).reshape(9 * filters, -1)]
  transfers between devices with their start and end apart: 2 -> 2, of which waited for: 1 -> 1; matrix products, arithmetic and copies ran while one was open for 1% -> 7% of each run, Pallas kernels for 0% -> 0%
where the time goes in v3:
time: 47.8 us; the launch traced here: 47.3 us
  Pallas kernels  33.8 us (71%)
  starting transfers between devices  5.37 us (11%)
  local copies, waits for them, and re-layouts  5.24 us (11%)
  other arithmetic  1.46 us (3%)
  waiting for transfers between devices  1.42 us (3%)
    pallas_call x1, Pallas kernels, gather_filt(): pl.pallas_call(functools.partial(gather_kernel, n), out_shape=jax.ShapeDt...  30.2 us
    pallas_call x1, Pallas kernels, conv_pool(): pl.pallas_call(functools.partial(conv_kernel, plane=plane, row=across, de...  3.56 us
    ppermute x1, starting transfers between devices, with_halo(): lax.ppermute(lax.slice_in_dim(block, block.shape[dim] - width, None, axis...  3.45 us
    ppermute x1, starting transfers between devices, with_halo(): lax.ppermute(lax.slice_in_dim(block, 0, width, axis=dim), axis, backward)  1.92 us
    ppermute x1, waiting for transfers between devices, with_halo(): lax.ppermute(lax.slice_in_dim(block, 0, width, axis=dim), axis, backward)  1.42 us
    reshape x1, local copies, waits for them, and re-layouts, conv_pool(): return out.reshape(filters, depth // 2, height // 2, across // 2)  1.39 us
    transpose x1, local copies, waits for them, and re-layouts, conv_pool(): weights = kernel.transpose(1, 2, 0, 3, 4).reshape(9 * filters, -1)  1.09 us
  transfers between devices with their start and end apart: 2, of which 1 were waited for; matrix products, arithmetic and copies ran while one was open for 7% of the time, Pallas kernels for 0%

profile of v3, /device:TPU:7, one launch (start us, length us, event | category | flops | bytes accessed | tf_op | source)
XLA Modules:
  0.0 47.3 jit_solution(10513688935111259319)
XLA Ops:
  0.0 0.7 %fusion = (bf16[8,1,4,128]{3,2,1,0:T(4,128)(2,1)S(1)}, bf16[8,1,4,128]{3,2,1,0:T(4,128)(2,1)S(1)}) fusion(bf16[8,4,4,128]{3,2,1,0:T(4,128)(2,1)} %param.3), kind=kLoop, calls=%fused_computation.2 | loop fusion | bytes 32768 | tf_op jit(solution)/shard_map/slice | solution.py:20
  0.7 3.5 %collective-permute-start = (bf16[8,1,4,128]{3,2,1,0:T(4,128)(2,1)S(1)}, bf16[8,1,4,128]{3,2,1,0:T(4,128)(2,1)S(1)}, u32[]{:S(2)}, u32[]{:S(2)}) collective-permute-start(bf16[8,1,4,128]{3,2,1,0:T(4,128)(2,1)S(1)} %get-tuple-element.5), channel_id=1, source_target_pairs={{0,1},{1,2},{2,3},{3,4},{4,5},{5,6},{6,7},{8,9},{9,10},{10,11},{11... | collective-permute-start | bytes 24584 | tf_op jit(solution)/shard_map/ppermute | solution.py:19
  4.2 1.9 %collective-permute-start.1 = (bf16[8,1,4,128]{3,2,1,0:T(4,128)(2,1)S(1)}, bf16[8,1,4,128]{3,2,1,0:T(4,128)(2,1)S(1)}, u32[]{:S(2)}, u32[]{:S(2)}) collective-permute-start(bf16[8,1,4,128]{3,2,1,0:T(4,128)(2,1)S(1)} %get-tuple-element.6), channel_id=1, source_target_pairs={{1,0},{2,1},{3,2},{4,3},{5,4},{6,5},{7,6},{9,8},{10,9},{11,10},{12... | collective-permute-start | bytes 24584 | tf_op jit(solution)/shard_map/ppermute | solution.py:22
  6.1 0.7 %bitcast_convert_fusion = f32[16,1]{0,1:T(1,128)S(1)} fusion(bf16[16]{0:T(256)(128)(2,1)} %param.5), kind=kLoop, calls=%fused_computation.1 | loop fusion | flops 16 | bytes 96 | tf_op jit(solution)/shard_map/reshape | solution.py:148
  6.8 0.7 %copy.7.b_ref = f32[16,1]{1,0:T(8,128)} copy(f32[16,1]{0,1:T(1,128)S(1)} %bitcast_convert_fusion) | data formatting | bytes 128 | tf_op jit(solution)/shard_map/reshape | solution.py:148
  7.5 1.1 %copy.6 = bf16[3,3,16,3,256]{4,3,2,1,0:T(4,128)(2,1)S(1)} copy(bf16[3,3,16,3,256]{4,2,3,1,0:T(8,128)(2,1)} %bitcast.9) | data formatting | bytes 442368 | tf_op jit(solution)/shard_map/transpose | solution.py:147
  8.5 0.7 %copy.8 = bf16[18,8,3,256]{3,1,2,0:T(8,128)(2,1)} copy(bf16[18,8,3,256]{3,2,1,0:T(4,128)(2,1)S(1)} %bitcast.7) | data formatting | bytes 442368
  9.3 0.0 collective-permute-done
  9.3 1.4 %collective-permute-done.1 = bf16[8,1,4,128]{3,2,1,0:T(4,128)(2,1)S(1)} collective-permute-done((bf16[8,1,4,128]{3,2,1,0:T(4,128)(2,1)S(1)}, bf16[8,1,4,128]{3,2,1,0:T(4,128)(2,1)S(1)}, u32[]{:S(2)}, u32[]{:S(2)}) %collective-permute-start.1) | collective-permute-done | bytes 8224 | tf_op jit(solution)/shard_map/ppermute | solution.py:22
  10.7 0.8 %pad_maximum_fusion = bf16[8,6,4,128]{3,2,1,0:T(4,128)(2,1)S(1)} fusion(bf16[8,1,4,128]{3,2,1,0:T(4,128)(2,1)S(1)} %collective-permute-done.1, bf16[8,4,4,128]{3,2,1,0:T(4,128)(2,1)} %param.3, bf16[8,1,4,128]{3,2,1,0:T(4,128)(2,1)S(1)} %collective-permute-done), kind=kLoop, calls=%fused_computation | loop fusion | flops 49152 | bytes 98304 | tf_op jit(solution)/shard_map/concatenate | solution.py:23
  11.5 0.6 %reshape.14.x_ref = bf16[8,3072]{1,0:T(8,128)(2,1)} reshape(bf16[8,6,4,128]{3,2,1,0:T(4,128)(2,1)S(1)} %pad_maximum_fusion) | data formatting | bytes 98304 | tf_op jit(solution)/shard_map/reshape | solution.py:162
  12.1 30.2 %shard_map.37.g_ref = bf16[256,3072]{1,0:T(8,128)(2,1)} custom-call(bf16[8,3072]{1,0:T(8,128)(2,1)} %reshape.14.x_ref), custom_call_target="tpu_custom_call" | custom-call | tf_op jit(solution)/shard_map/pallas_call | solution.py:80
  42.4 3.6 %shard_map.38 = bf16[16,256]{1,0:T(8,128)(2,1)} custom-call(bf16[256,3072]{1,0:T(8,128)(2,1)} %shard_map.37.g_ref, bf16[144,768]{1,0:T(8,128)(2,1)} %bitcast.8, f32[16,1]{1,0:T(8,128)} %copy.7.b_ref), custom_call_target="tpu_custom_call" | custom-call | tf_op jit(solution)/shard_map/pallas_call | solution.py:150
  45.9 1.4 %reshape.18 = bf16[16,2,2,64]{3,2,1,0:T(2,128)(2,1)} reshape(bf16[16,256]{1,0:T(8,128)(2,1)} %shard_map.38) | data formatting | bytes 16384 | tf_op jit(solution)/shard_map/reshape | solution.py:156
Async XLA Ops:
  0.7 8.5 %collective-permute-start = (bf16[8,1,4,128]{3,2,1,0:T(4,128)(2,1)S(1)}, bf16[8,1,4,128]{3,2,1,0:T(4,128)(2,1)S(1)}, u32[]{:S(2)}, u32[]{:S(2)}) collective-permute-start(bf16[8,1,4,128]{3,2,1,0:T(4,128)(2,1)S(1)} %get-tuple-element.5), channel_id=1, source_target_pairs={{0,1},{1,2},{2,3},{3,4},{4,5},{5,6},{6,7},{8,9},{9,10},{10,11},{11... | collective-permute-start | bytes 24584 | tf_op jit(solution)/shard_map/ppermute | solution.py:19
  4.2 6.5 %collective-permute-start.1 = (bf16[8,1,4,128]{3,2,1,0:T(4,128)(2,1)S(1)}, bf16[8,1,4,128]{3,2,1,0:T(4,128)(2,1)S(1)}, u32[]{:S(2)}, u32[]{:S(2)}) collective-permute-start(bf16[8,1,4,128]{3,2,1,0:T(4,128)(2,1)S(1)} %get-tuple-element.6), channel_id=1, source_target_pairs={{1,0},{2,1},{3,2},{4,3},{5,4},{6,5},{7,6},{9,8},{10,9},{11,10},{12... | collective-permute-start | bytes 24584 | tf_op jit(solution)/shard_map/ppermute | solution.py:22

commit v4 on v3

v4 whole, which is shorter than its diff:
```python
import functools

import jax
import jax.numpy as jnp
from jax import lax
from jax.experimental import pallas as pl
from jax.experimental.pallas import tpu as pltpu
from jax.sharding import PartitionSpec as P

slope = 0.3
MESH = pl.DeviceIdType.MESH


def gather_kernel(n, slabs, x_ref, out_ref, local_sem, send_sem, fwd_sem, halo_sem,
                  recv_sem, lo_sem, hi_sem):
    me = lax.axis_index("filt")
    sp = lax.axis_index("space")
    chips = n // 2
    core = lax.rem(me, 2)
    chip = me // 2
    sib = me + 1 - 2 * core
    peers = [lax.rem(chip + k, chips) * 2 + core for k in range(1, chips)]
    sources = [lax.rem(chip + chips - k, chips) * 2 + core for k in range(1, chips)]
    rows, cols = x_ref.shape
    plane = cols // 4
    has_lo = sp > 0
    has_hi = sp < slabs - 1

    def rows_of(slot):
        return pl.ds(pl.multiple_of(slot * rows, rows), rows)

    def main_at(slot):
        return out_ref.at[rows_of(slot), pl.ds(plane, cols)]

    def lo_at(slot):
        return out_ref.at[rows_of(slot), pl.ds(0, plane)]

    def hi_at(slot):
        return out_ref.at[rows_of(slot), pl.ds(plane + cols, plane)]

    barrier = pltpu.get_barrier_semaphore()
    for peer in [sib] + peers:
        pl.semaphore_signal(barrier, inc=1, device_id=(peer, sp), device_id_type=MESH)

    @pl.when(has_lo)
    def _():
        pl.semaphore_signal(barrier, inc=1, device_id=(me, sp - 1), device_id_type=MESH)

    @pl.when(has_hi)
    def _():
        pl.semaphore_signal(barrier, inc=1, device_id=(me, sp + 1), device_id_type=MESH)

    pl.semaphore_wait(barrier, chips + has_lo.astype(jnp.int32) + has_hi.astype(jnp.int32))

    def copy(src, dst, sem, recv, dev):
        return pltpu.make_async_remote_copy(
            src_ref=src, dst_ref=dst, send_sem=sem, recv_sem=recv,
            device_id=dev, device_id_type=MESH,
        )

    def main_copy(src, slot, sem, dev):
        return copy(src, main_at(slot), sem, recv_sem.at[slot], (dev, sp))

    def halo_out(src_rows, slot, k):
        down = copy(src_rows(0), hi_at(slot), halo_sem.at[0, k], hi_sem.at[slot], (me, sp - 1))
        up = copy(src_rows(3), lo_at(slot), halo_sem.at[1, k], lo_sem.at[slot], (me, sp + 1))

        @pl.when(has_lo)
        def _():
            down.start()

        @pl.when(has_hi)
        def _():
            up.start()

        return down, up

    local = pltpu.make_async_copy(x_ref, main_at(me), local_sem.at[0])
    local.start()
    sends = [main_copy(x_ref, me, send_sem.at[0], sib)]
    for k, peer in enumerate(peers):
        sends.append(main_copy(x_ref, me, send_sem.at[k + 1], peer))
    for c in sends:
        c.start()
    halos = [halo_out(lambda p: x_ref.at[:, pl.ds(p * plane, plane)], me, 0)]
    forwards = []
    for k, src in enumerate(sources):
        main_copy(main_at(src), src, fwd_sem.at[0, k], src).wait_recv()
        c = main_copy(main_at(src), src, fwd_sem.at[0, k], sib)
        c.start()
        forwards.append(c)
        held = lambda p, src=src: out_ref.at[rows_of(src), pl.ds((p + 1) * plane, plane)]
        halos.append(halo_out(held, src, k + 1))
    same_core = [me] + sources
    lo_fwd, hi_fwd = [], []
    for k, src in enumerate(same_core):
        lo = copy(lo_at(src), lo_at(src), fwd_sem.at[1, k], lo_sem.at[src], (sib, sp))
        hi = copy(hi_at(src), hi_at(src), fwd_sem.at[2, k], hi_sem.at[src], (sib, sp))

        @pl.when(has_lo)
        def _():
            lo.wait_recv()
            lo.start()

        @pl.when(has_hi)
        def _():
            hi.wait_recv()
            hi.start()

        lo_fwd.append(lo)
        hi_fwd.append(hi)
    main_copy(main_at(sib), sib, send_sem.at[0], sib).wait_recv()
    for k in range(1, chips):
        src = lax.rem(chip + chips - k, chips) * 2 + 1 - core
        main_copy(main_at(src), src, fwd_sem.at[0, k - 1], sib).wait_recv()
    other_core = [sib] + [lax.rem(chip + chips - k, chips) * 2 + 1 - core for k in range(1, chips)]
    for k, src in enumerate(other_core):
        lo = copy(lo_at(src), lo_at(src), fwd_sem.at[1, k], lo_sem.at[src], (sib, sp))
        hi = copy(hi_at(src), hi_at(src), fwd_sem.at[2, k], hi_sem.at[src], (sib, sp))

        @pl.when(has_lo)
        def _():
            lo.wait_recv()

        @pl.when(has_hi)
        def _():
            hi.wait_recv()

    for c in sends + forwards:
        c.wait_send()
    for down, up in halos:
        @pl.when(has_lo)
        def _():
            down.wait_send()

        @pl.when(has_hi)
        def _():
            up.wait_send()

    for lo, hi in zip(lo_fwd, hi_fwd):
        @pl.when(has_lo)
        def _():
            lo.wait_send()

        @pl.when(has_hi)
        def _():
            hi.wait_send()

    local.wait()


def gather_filt(block):
    n = lax.axis_size("filt")
    slabs = lax.axis_size("space")
    rows, cols = block.shape
    chips = n // 2
    return pl.pallas_call(
        functools.partial(gather_kernel, n, slabs),
        out_shape=jax.ShapeDtypeStruct((n * rows, cols + cols // 2), block.dtype),
        in_specs=[pl.BlockSpec(memory_space=pl.ANY)],
        out_specs=pl.BlockSpec(memory_space=pl.ANY),
        scratch_shapes=[
            pltpu.SemaphoreType.DMA((1,)),
            pltpu.SemaphoreType.DMA((chips,)),
            pltpu.SemaphoreType.DMA((3, chips)),
            pltpu.SemaphoreType.DMA((2, chips)),
            pltpu.SemaphoreType.DMA((n,)),
            pltpu.SemaphoreType.DMA((n,)),
            pltpu.SemaphoreType.DMA((n,)),
        ],
        compiler_params=pltpu.CompilerParams(collective_id=0, has_side_effects=True),
    )(block)


def conv_kernel(g_ref, w_ref, b_ref, o_ref, *, plane, row, depth, slabs):
    sp = lax.axis_index("space")
    g = g_ref[...]
    cols = g.shape[1]
    col = lax.broadcasted_iota(jnp.int32, g.shape, 1)
    zero = jnp.zeros_like(g)
    edge = ((col < plane) & (sp == 0)) | ((col >= cols - plane) & (sp == slabs - 1))
    g = jnp.where(edge, zero, g)
    x = col % row
    left = jnp.where(x == 0, zero, pltpu.roll(g, 1, 1))
    right = jnp.where(x == row - 1, zero, pltpu.roll(g, cols - 1, 1))
    stacked = jnp.concatenate([left, g, right], axis=0)
    weights = jnp.concatenate(
        [jnp.concatenate([w_ref[a, b, c] for c in range(3)], axis=1)
         for a in range(3) for b in range(3)],
        axis=0,
    )
    q = jnp.dot(weights, stacked, preferred_element_type=jnp.float32)
    filters = w_ref.shape[3]
    out_cols = depth * plane
    acc = jnp.zeros((filters, out_cols), jnp.float32)
    for a in range(3):
        for b in range(3):
            tap = q[(a * 3 + b) * filters:(a * 3 + b + 1) * filters]
            shift = a * plane + (b - 1) * row
            if b == 1:
                acc = acc + tap[:, shift:shift + out_cols]
                continue
            pieces = []
            for z in range(depth):
                lo = z * plane + (row if b == 0 else 0)
                hi = lo + plane - row
                part = tap[:, lo + shift:hi + shift]
                pad = jnp.zeros((filters, row), jnp.float32)
                pieces += [pad, part] if b == 0 else [part, pad]
            acc = acc + jnp.concatenate(pieces, axis=1)
    pooled = []
    for zp in range(depth // 2):
        zmax = jnp.maximum(
            acc[:, 2 * zp * plane:(2 * zp + 1) * plane],
            acc[:, (2 * zp + 1) * plane:(2 * zp + 2) * plane],
        )
        for yp in range(plane // row // 2):
            pooled.append(
                jnp.maximum(
                    zmax[:, 2 * yp * row:(2 * yp + 1) * row],
                    zmax[:, (2 * yp + 1) * row:(2 * yp + 2) * row],
                )
            )
    m = jnp.concatenate(pooled, axis=1)
    m = jnp.maximum(m, pltpu.roll(m, m.shape[1] - 1, 1))
    brow = jnp.broadcast_to(b_ref[...].astype(jnp.float32), (filters, filters))
    r16 = lax.broadcasted_iota(jnp.int32, (filters, filters), 0)
    c16 = lax.broadcasted_iota(jnp.int32, (filters, filters), 1)
    bias = jnp.sum(jnp.where(r16 == c16, brow, 0.0), axis=1, keepdims=True)
    v = m + bias
    v = jnp.where(v > 0, v, slope * v).astype(jnp.bfloat16)
    r = lax.broadcasted_iota(jnp.int32, (m.shape[1], m.shape[1] // 2), 0)
    c = lax.broadcasted_iota(jnp.int32, (m.shape[1], m.shape[1] // 2), 1)
    pick = (r == 2 * c).astype(jnp.bfloat16)
    o_ref[...] = jnp.dot(v, pick, preferred_element_type=jnp.float32).astype(o_ref.dtype)


def conv_pool(gathered, kernel, filter_bias, depth, height, across):
    filters = kernel.shape[0]
    weights = kernel.transpose(1, 2, 3, 0, 4)
    bias = filter_bias.reshape(1, filters)
    plane = height * across
    out = pl.pallas_call(
        functools.partial(conv_kernel, plane=plane, row=across, depth=depth,
                          slabs=lax.axis_size("space")),
        out_shape=jax.ShapeDtypeStruct((filters, depth * plane // 8), jnp.bfloat16),
        in_specs=[pl.BlockSpec(memory_space=pltpu.VMEM)] * 3,
        out_specs=pl.BlockSpec(memory_space=pltpu.VMEM),
    )(gathered, weights, bias)
    return out.reshape(filters, depth // 2, height // 2, across // 2)


def on_device(volume, kernel, filter_bias):
    local_in, depth, height, across = volume.shape
    gathered = gather_filt(volume.reshape(local_in, -1))
    return conv_pool(gathered, kernel, filter_bias, depth, height, across)


def solution(mesh):
    in_specs = (P("filt", "space", None, None), P("filt", None, None, None, None), P("filt"))
    out_specs = P("filt", "space", None, None)
    return jax.shard_map(
        on_device, mesh=mesh, in_specs=in_specs, out_specs=out_specs, check_vma=False
    )
```

time: 47.8 us -> 37.4 us (0.78)
  the two profiles are of different devices: /device:TPU:7 before, /device:TPU:33 now
where the time goes in v4:
time: 37.4 us; the launch traced here: 37.1 us
  Pallas kernels  34.4 us (92%)
  local copies, waits for them, and re-layouts  2.76 us (7%)
    pallas_call x1, Pallas kernels, gather_filt(): pl.pallas_call(functools.partial(gather_kernel, n, slabs), out_shape=jax....  30.8 us
    pallas_call x1, Pallas kernels, conv_pool(): pl.pallas_call(functools.partial(conv_kernel, plane=plane, row=across, de...  3.6 us
    reshape x1, local copies, waits for them, and re-layouts, conv_pool(): return out.reshape(filters, depth // 2, height // 2, across // 2)  1.39 us
    reshape x1, local copies, waits for them, and re-layouts, on_device(): gathered = gather_filt(volume.reshape(local_in, -1))  1.37 us

profile of v4, /device:TPU:33, one launch (start us, length us, event | category | flops | bytes accessed | tf_op | source)
XLA Modules:
  0.0 37.1 jit_solution(13681687076850650127)
XLA Ops:
  0.0 1.4 %reshape.9.x_ref = bf16[8,2048]{1,0:T(8,128)(2,1)} reshape(bf16[8,4,4,128]{3,2,1,0:T(4,128)(2,1)} %param.3) | data formatting | bytes 65536 | tf_op jit(solution)/shard_map/reshape | solution.py:255
  1.4 30.8 %shard_map.37.g_ref = bf16[256,3072]{1,0:T(8,128)(2,1)} custom-call(bf16[8,2048]{1,0:T(8,128)(2,1)} %reshape.9.x_ref), custom_call_target="tpu_custom_call" | custom-call | tf_op jit(solution)/shard_map/pallas_call | solution.py:157
  32.2 3.6 %shard_map.38 = bf16[16,256]{1,0:T(8,128)(2,1)} custom-call(bf16[256,3072]{1,0:T(8,128)(2,1)} %shard_map.37.g_ref, bf16[3,3,3,16,256]{4,3,2,1,0:T(8,128)(2,1)} %bitcast.2, bf16[1,16]{1,0:T(2,128)(2,1)} %bitcast.3), custom_call_target="tpu_custom_call" | custom-call | tf_op jit(solution)/shard_map/pallas_call | solution.py:243
  35.8 1.4 %reshape.11 = bf16[16,2,2,64]{3,2,1,0:T(2,128)(2,1)} reshape(bf16[16,256]{1,0:T(8,128)(2,1)} %shard_map.38) | data formatting | bytes 16384 | tf_op jit(solution)/shard_map/reshape | solution.py:250

commit v5 on v4

--- a/solution.py
+++ b/solution.py
@@ -11,8 +11,13 @@
 MESH = pl.DeviceIdType.MESH
 
 
-def gather_kernel(n, slabs, x_ref, out_ref, local_sem, send_sem, fwd_sem, halo_sem,
+def gather_kernel(n, slabs, v_ref, out_ref, x_ref, local_sem, send_sem, fwd_sem, halo_sem,
                   recv_sem, lo_sem, hi_sem):
+    depth, height = v_ref.shape[1], v_ref.shape[2]
+    across = v_ref.shape[3]
+    for z in range(depth):
+        for y in range(height):
+            x_ref[:, pl.ds((z * height + y) * across, across)] = v_ref[:, z, y, :]
     me = lax.axis_index("filt")
     sp = lax.axis_index("space")
     chips = n // 2
@@ -152,14 +157,16 @@
 def gather_filt(block):
     n = lax.axis_size("filt")
     slabs = lax.axis_size("space")
-    rows, cols = block.shape
+    rows = block.shape[0]
+    cols = block.size // rows
     chips = n // 2
     return pl.pallas_call(
         functools.partial(gather_kernel, n, slabs),
         out_shape=jax.ShapeDtypeStruct((n * rows, cols + cols // 2), block.dtype),
-        in_specs=[pl.BlockSpec(memory_space=pl.ANY)],
+        in_specs=[pl.BlockSpec(memory_space=pltpu.VMEM)],
         out_specs=pl.BlockSpec(memory_space=pl.ANY),
         scratch_shapes=[
+            pltpu.VMEM((rows, cols), block.dtype),
             pltpu.SemaphoreType.DMA((1,)),
             pltpu.SemaphoreType.DMA((chips,)),
             pltpu.SemaphoreType.DMA((3, chips)),
@@ -232,7 +239,12 @@
     r = lax.broadcasted_iota(jnp.int32, (m.shape[1], m.shape[1] // 2), 0)
     c = lax.broadcasted_iota(jnp.int32, (m.shape[1], m.shape[1] // 2), 1)
     pick = (r == 2 * c).astype(jnp.bfloat16)
-    o_ref[...] = jnp.dot(v, pick, preferred_element_type=jnp.float32).astype(o_ref.dtype)
+    picked = jnp.dot(v, pick, preferred_element_type=jnp.float32).astype(o_ref.dtype)
+    half = row // 2
+    for zp in range(o_ref.shape[1]):
+        for yp in range(o_ref.shape[2]):
+            k = zp * o_ref.shape[2] + yp
+            o_ref[:, zp, yp, :] = picked[:, k * half:(k + 1) * half]
 
 
 def conv_pool(gathered, kernel, filter_bias, depth, height, across):
@@ -243,16 +255,16 @@
     out = pl.pallas_call(
         functools.partial(conv_kernel, plane=plane, row=across, depth=depth,
                           slabs=lax.axis_size("space")),
-        out_shape=jax.ShapeDtypeStruct((filters, depth * plane // 8), jnp.bfloat16),
+        out_shape=jax.ShapeDtypeStruct((filters, depth // 2, height // 2, across // 2), jnp.bfloat16),
         in_specs=[pl.BlockSpec(memory_space=pltpu.VMEM)] * 3,
         out_specs=pl.BlockSpec(memory_space=pltpu.VMEM),
     )(gathered, weights, bias)
-    return out.reshape(filters, depth // 2, height // 2, across // 2)
+    return out
 
 
 def on_device(volume, kernel, filter_bias):
     local_in, depth, height, across = volume.shape
-    gathered = gather_filt(volume.reshape(local_in, -1))
+    gathered = gather_filt(volume)
     return conv_pool(gathered, kernel, filter_bias, depth, height, across)
 
 

time: 37.4 us -> 35.1 us (0.939)
  local copies, waits for them, and re-layouts: 2.76 us -> 0 us
  Pallas kernels: 34.4 us -> 34.9 us
    reshape x2 -> x0, local copies, waits for them, and re-layouts: 2.76 us -> none  [the longest x1 1.39 us: conv_pool(): return out.reshape(filters, depth // 2, height // 2, across // 2)]
    pallas_call x1, Pallas kernels: 30.8 us -> 31.3 us  [gather_filt(): pl.pallas_call(functools.partial(gather_kernel, n, slabs), out_shape=jax....]
where the time goes in v5:
time: 35.1 us; the launch traced here: 34.9 us
  Pallas kernels  34.9 us (99%)
    pallas_call x1, Pallas kernels, gather_filt(): pl.pallas_call(functools.partial(gather_kernel, n, slabs), out_shape=jax....  31.3 us
    pallas_call x1, Pallas kernels, conv_pool(): pl.pallas_call(functools.partial(conv_kernel, plane=plane, row=across, de...  3.67 us

profile of v5, /device:TPU:33, one launch (start us, length us, event | category | flops | bytes accessed | tf_op | source)
XLA Modules:
  0.0 34.9 jit_solution(4985434799533083422)
XLA Ops:
  0.0 31.3 %shard_map.37.g_ref = bf16[256,3072]{1,0:T(8,128)(2,1)} custom-call(bf16[8,4,4,128]{3,2,1,0:T(4,128)(2,1)} %v_ref.1), custom_call_target="tpu_custom_call" | custom-call | tf_op jit(solution)/shard_map/pallas_call | solution.py:163
  31.3 3.7 %shard_map.38 = bf16[16,2,2,64]{3,2,1,0:T(2,128)(2,1)} custom-call(bf16[256,3072]{1,0:T(8,128)(2,1)} %shard_map.37.g_ref, bf16[3,3,3,16,256]{4,3,2,1,0:T(8,128)(2,1)} %bitcast.2, bf16[1,16]{1,0:T(2,128)(2,1)} %bitcast.3), custom_call_target="tpu_custom_call" | custom-call | tf_op jit(solution)/shard_map/pallas_call | solution.py:255

commit v6 on v5

--- a/solution.py
+++ b/solution.py
@@ -11,23 +11,31 @@
 MESH = pl.DeviceIdType.MESH
 
 
-def gather_kernel(n, slabs, v_ref, out_ref, x_ref, local_sem, send_sem, fwd_sem, halo_sem,
-                  recv_sem, lo_sem, hi_sem):
-    depth, height = v_ref.shape[1], v_ref.shape[2]
-    across = v_ref.shape[3]
+def gather_kernel(n, slabs, v_ref, out_ref, x_ref, local_sem, send_sem, fwd_sem, relay_sem,
+                  halo_sem, recv_sem, lo_sem, hi_sem):
+    depth, height, across = v_ref.shape[1:]
     for z in range(depth):
         for y in range(height):
             x_ref[:, pl.ds((z * height + y) * across, across)] = v_ref[:, z, y, :]
     me = lax.axis_index("filt")
     sp = lax.axis_index("space")
     chips = n // 2
+    zn = 4
+    yn = chips // zn
     core = lax.rem(me, 2)
     chip = me // 2
+    yy, zz = chip // zn, lax.rem(chip, zn)
     sib = me + 1 - 2 * core
-    peers = [lax.rem(chip + k, chips) * 2 + core for k in range(1, chips)]
-    sources = [lax.rem(chip + chips - k, chips) * 2 + core for k in range(1, chips)]
+
+    def dev(dy, dz):
+        return (lax.rem(yy + dy + yn, yn) * zn + lax.rem(zz + dz + zn, zn)) * 2 + core
+
+    direct = [(dy, dz) for dz in (1, 3, 0) for dy in range(yn) if (dy, dz) != (0, 0)]
+    far = [(dy, 2) for dy in range(yn)]
+    peers = [dev(dy, dz) for dy, dz in direct]
     rows, cols = x_ref.shape
-    plane = cols // 4
+    plane = cols // depth
+    half = cols // 2
     has_lo = sp > 0
     has_hi = sp < slabs - 1
 
@@ -55,20 +63,23 @@
     def _():
         pl.semaphore_signal(barrier, inc=1, device_id=(me, sp + 1), device_id_type=MESH)
 
-    pl.semaphore_wait(barrier, chips + has_lo.astype(jnp.int32) + has_hi.astype(jnp.int32))
-
-    def copy(src, dst, sem, recv, dev):
+    pl.semaphore_wait(
+        barrier, 1 + len(peers) + has_lo.astype(jnp.int32) + has_hi.astype(jnp.int32)
+    )
+
+    def copy(src, dst, sem, recv, dev_id):
         return pltpu.make_async_remote_copy(
             src_ref=src, dst_ref=dst, send_sem=sem, recv_sem=recv,
-            device_id=dev, device_id_type=MESH,
+            device_id=dev_id, device_id_type=MESH,
         )
 
-    def main_copy(src, slot, sem, dev):
-        return copy(src, main_at(slot), sem, recv_sem.at[slot], (dev, sp))
+    def main_copy(src, slot, sem, dev_id):
+        return copy(src, main_at(slot), sem, recv_sem.at[slot], (dev_id, sp))
 
     def halo_out(src_rows, slot, k):
         down = copy(src_rows(0), hi_at(slot), halo_sem.at[0, k], hi_sem.at[slot], (me, sp - 1))
-        up = copy(src_rows(3), lo_at(slot), halo_sem.at[1, k], lo_sem.at[slot], (me, sp + 1))
+        up = copy(src_rows(depth - 1), lo_at(slot), halo_sem.at[1, k], lo_sem.at[slot],
+                  (me, sp + 1))
 
         @pl.when(has_lo)
         def _():
@@ -89,13 +100,24 @@
         c.start()
     halos = [halo_out(lambda p: x_ref.at[:, pl.ds(p * plane, plane)], me, 0)]
     forwards = []
-    for k, src in enumerate(sources):
+    relays = []
+    sources = []
+    for k, (dy, dz) in enumerate(direct + far):
+        src = dev(-dy, -dz)
+        sources.append(src)
         main_copy(main_at(src), src, fwd_sem.at[0, k], src).wait_recv()
+        if dz in (1, 3):
+            part = pl.ds(plane + (0 if dz == 1 else half), half)
+            held = out_ref.at[rows_of(src), part]
+            target = dev(0, 1 if dz == 1 else -1)
+            r = copy(held, held, relay_sem.at[dz // 2, dy], recv_sem.at[src], (target, sp))
+            r.start()
+            relays.append(r)
         c = main_copy(main_at(src), src, fwd_sem.at[0, k], sib)
         c.start()
         forwards.append(c)
-        held = lambda p, src=src: out_ref.at[rows_of(src), pl.ds((p + 1) * plane, plane)]
-        halos.append(halo_out(held, src, k + 1))
+        held_plane = lambda p, src=src: out_ref.at[rows_of(src), pl.ds((p + 1) * plane, plane)]
+        halos.append(halo_out(held_plane, src, k + 1))
     same_core = [me] + sources
     lo_fwd, hi_fwd = [], []
     for k, src in enumerate(same_core):
@@ -114,12 +136,9 @@
 
         lo_fwd.append(lo)
         hi_fwd.append(hi)
-    main_copy(main_at(sib), sib, send_sem.at[0], sib).wait_recv()
-    for k in range(1, chips):
-        src = lax.rem(chip + chips - k, chips) * 2 + 1 - core
-        main_copy(main_at(src), src, fwd_sem.at[0, k - 1], sib).wait_recv()
-    other_core = [sib] + [lax.rem(chip + chips - k, chips) * 2 + 1 - core for k in range(1, chips)]
+    other_core = [s + 1 - 2 * core for s in same_core]
     for k, src in enumerate(other_core):
+        main_copy(main_at(src), src, fwd_sem.at[0, 0], sib).wait_recv()
         lo = copy(lo_at(src), lo_at(src), fwd_sem.at[1, k], lo_sem.at[src], (sib, sp))
         hi = copy(hi_at(src), hi_at(src), fwd_sem.at[2, k], hi_sem.at[src], (sib, sp))
 
@@ -131,7 +150,7 @@
         def _():
             hi.wait_recv()
 
-    for c in sends + forwards:
+    for c in sends + forwards + relays:
         c.wait_send()
     for down, up in halos:
         @pl.when(has_lo)
@@ -170,6 +189,7 @@
             pltpu.SemaphoreType.DMA((1,)),
             pltpu.SemaphoreType.DMA((chips,)),
             pltpu.SemaphoreType.DMA((3, chips)),
+            pltpu.SemaphoreType.DMA((2, chips // 4)),
             pltpu.SemaphoreType.DMA((2, chips)),
             pltpu.SemaphoreType.DMA((n,)),
             pltpu.SemaphoreType.DMA((n,)),

time: 35.1 us -> 34.5 us (0.983)
  the two profiles are of different devices: /device:TPU:33 before, /device:TPU:7 now
where the time goes in v6:
time: 34.5 us; the launch traced here: 34.1 us
  Pallas kernels  34.1 us (99%)
    pallas_call x1, Pallas kernels, gather_filt(): pl.pallas_call(functools.partial(gather_kernel, n, slabs), out_shape=jax....  30.4 us
    pallas_call x1, Pallas kernels, conv_pool(): pl.pallas_call(functools.partial(conv_kernel, plane=plane, row=across, de...  3.68 us

profile of v6, /device:TPU:7, one launch (start us, length us, event | category | flops | bytes accessed | tf_op | source)
XLA Modules:
  0.0 34.1 jit_solution(12740833759905521313)
XLA Ops:
  0.0 30.4 %shard_map.37.g_ref = bf16[256,3072]{1,0:T(8,128)(2,1)} custom-call(bf16[8,4,4,128]{3,2,1,0:T(4,128)(2,1)} %v_ref.1), custom_call_target="tpu_custom_call" | custom-call | tf_op jit(solution)/shard_map/pallas_call | solution.py:182
  30.4 3.7 %shard_map.38 = bf16[16,2,2,64]{3,2,1,0:T(2,128)(2,1)} custom-call(bf16[256,3072]{1,0:T(8,128)(2,1)} %shard_map.37.g_ref, bf16[3,3,3,16,256]{4,3,2,1,0:T(8,128)(2,1)} %bitcast.2, bf16[1,16]{1,0:T(2,128)(2,1)} %bitcast.3), custom_call_target="tpu_custom_call" | custom-call | tf_op jit(solution)/shard_map/pallas_call | solution.py:275

commit v7 on v6

v7 whole, which is shorter than its diff:
```python
import functools

import jax
import jax.numpy as jnp
from jax import lax
from jax.experimental import pallas as pl
from jax.experimental.pallas import tpu as pltpu
from jax.sharding import PartitionSpec as P

slope = 0.3
MESH = pl.DeviceIdType.MESH


def gather_kernel(n, v_ref, out_ref, x_ref, local_sem, send_sem, fwd_sem, relay_sem, recv_sem):
    depth, height, across = v_ref.shape[1:]
    for z in range(depth):
        for y in range(height):
            x_ref[:, pl.ds((z * height + y) * across, across)] = v_ref[:, z, y, :]
    me = lax.axis_index("filt")
    sp = lax.axis_index("space")
    chips = n // 2
    zn = 4
    yn = chips // zn
    core = lax.rem(me, 2)
    chip = me // 2
    yy, zz = chip // zn, lax.rem(chip, zn)
    sib = me + 1 - 2 * core

    def dev(dy, dz):
        return (lax.rem(yy + dy + yn, yn) * zn + lax.rem(zz + dz + zn, zn)) * 2 + core

    direct = [(dy, dz) for dz in (1, 3, 0) for dy in range(yn) if (dy, dz) != (0, 0)]
    far = [(dy, 2) for dy in range(yn)]
    peers = [dev(dy, dz) for dy, dz in direct]
    rows, cols = x_ref.shape
    plane = cols // depth
    half = cols // 2

    def rows_of(slot):
        return pl.ds(pl.multiple_of(slot * rows, rows), rows)

    def main_at(slot):
        return out_ref.at[rows_of(slot)]

    barrier = pltpu.get_barrier_semaphore()
    for peer in [sib] + peers:
        pl.semaphore_signal(barrier, inc=1, device_id=(peer, sp), device_id_type=MESH)
    pl.semaphore_wait(barrier, 1 + len(peers))

    def copy(src, dst, sem, recv, dev_id):
        return pltpu.make_async_remote_copy(
            src_ref=src, dst_ref=dst, send_sem=sem, recv_sem=recv,
            device_id=dev_id, device_id_type=MESH,
        )

    def main_copy(src, slot, sem, dev_id):
        return copy(src, main_at(slot), sem, recv_sem.at[slot], (dev_id, sp))

    local = pltpu.make_async_copy(x_ref, main_at(me), local_sem.at[0])
    local.start()
    sends = [main_copy(x_ref, me, send_sem.at[0], sib)]
    for k, peer in enumerate(peers):
        sends.append(main_copy(x_ref, me, send_sem.at[k + 1], peer))
    for c in sends:
        c.start()
    forwards = []
    relays = []
    sources = []
    for k, (dy, dz) in enumerate(direct + far):
        src = dev(-dy, -dz)
        sources.append(src)
        main_copy(main_at(src), src, fwd_sem.at[0, k], src).wait_recv()
        if dz in (1, 3):
            part = pl.ds(0 if dz == 1 else half, half)
            held = out_ref.at[rows_of(src), part]
            target = dev(0, 1 if dz == 1 else -1)
            r = copy(held, held, relay_sem.at[dz // 2, dy], recv_sem.at[src], (target, sp))
            r.start()
            relays.append(r)
        c = main_copy(main_at(src), src, fwd_sem.at[0, k], sib)
        c.start()
        forwards.append(c)
    for k in range(chips):
        src = (sources[k - 1] if k else me) + 1 - 2 * core
        main_copy(main_at(src), src, fwd_sem.at[0, 0], sib).wait_recv()
    for c in sends + forwards + relays:
        c.wait_send()
    local.wait()


def gather_filt(block):
    n = lax.axis_size("filt")
    rows = block.shape[0]
    cols = block.size // rows
    chips = n // 2
    return pl.pallas_call(
        functools.partial(gather_kernel, n),
        out_shape=jax.ShapeDtypeStruct((n * rows, cols), block.dtype),
        in_specs=[pl.BlockSpec(memory_space=pltpu.VMEM)],
        out_specs=pl.BlockSpec(memory_space=pl.ANY),
        scratch_shapes=[
            pltpu.VMEM((rows, cols), block.dtype),
            pltpu.SemaphoreType.DMA((1,)),
            pltpu.SemaphoreType.DMA((chips,)),
            pltpu.SemaphoreType.DMA((1, chips)),
            pltpu.SemaphoreType.DMA((2, chips // 4)),
            pltpu.SemaphoreType.DMA((n,)),
        ],
        compiler_params=pltpu.CompilerParams(collective_id=0, has_side_effects=True),
    )(block)


def conv_kernel(g_ref, w_ref, b_ref, o_ref, send_buf, recv_buf, send_sem, recv_sem, *,
                plane, row, depth, slabs):
    sp = lax.axis_index("space")
    me = lax.axis_index("filt")
    has_lo = sp > 0
    has_hi = sp < slabs - 1
    g = g_ref[...]
    cols = g.shape[1]
    heights = plane // row
    x = lax.broadcasted_iota(jnp.int32, g.shape, 1) % row
    zero = jnp.zeros_like(g)
    left = jnp.where(x == 0, zero, pltpu.roll(g, 1, 1))
    right = jnp.where(x == row - 1, zero, pltpu.roll(g, cols - 1, 1))
    stacked = jnp.concatenate([left, g, right], axis=0)
    weights = jnp.concatenate(
        [jnp.concatenate([w_ref[a, b, c] for c in range(3)], axis=1)
         for a in range(3) for b in range(3)],
        axis=0,
    )
    q = jnp.dot(weights, stacked, preferred_element_type=jnp.float32)
    filters = w_ref.shape[3]

    def tap_row(a, b, p, y):
        if not 0 <= y < heights:
            return None
        t = (a * 3 + b) * filters
        c0 = p * plane + y * row
        return q[t:t + filters, c0:c0 + row]

    def plane_sum(a, p):
        out = []
        for y in range(heights):
            parts = [tap_row(a, b, p, y + b - 1) for b in range(3)]
            parts = [v for v in parts if v is not None]
            total = parts[0]
            for v in parts[1:]:
                total = total + v
            out.append(total)
        return out

    send_buf[0] = jnp.concatenate(plane_sum(0, depth - 1), axis=1)
    send_buf[1] = jnp.concatenate(plane_sum(2, 0), axis=1)
    barrier = pltpu.get_barrier_semaphore()

    @pl.when(has_lo)
    def _():
        pl.semaphore_signal(barrier, inc=1, device_id=(me, sp - 1), device_id_type=MESH)

    @pl.when(has_hi)
    def _():
        pl.semaphore_signal(barrier, inc=1, device_id=(me, sp + 1), device_id_type=MESH)

    pl.semaphore_wait(barrier, has_lo.astype(jnp.int32) + has_hi.astype(jnp.int32))
    up = pltpu.make_async_remote_copy(
        src_ref=send_buf.at[0], dst_ref=recv_buf.at[0], send_sem=send_sem.at[0],
        recv_sem=recv_sem.at[0], device_id=(me, sp + 1), device_id_type=MESH,
    )
    down = pltpu.make_async_remote_copy(
        src_ref=send_buf.at[1], dst_ref=recv_buf.at[1], send_sem=send_sem.at[1],
        recv_sem=recv_sem.at[1], device_id=(me, sp - 1), device_id_type=MESH,
    )

    @pl.when(has_hi)
    def _():
        up.start()

    @pl.when(has_lo)
    def _():
        down.start()

    acc = []
    for z in range(depth):
        rows_z = None
        for a in range(3):
            p = z + a - 1
            if not 0 <= p < depth:
                continue
            part = plane_sum(a, p)
            rows_z = part if rows_z is None else [u + v for u, v in zip(rows_z, part)]
        acc.append(rows_z)

    @pl.when(has_hi)
    def _():
        up.wait_send()
        down_recv = pltpu.make_async_remote_copy(
            src_ref=send_buf.at[1], dst_ref=recv_buf.at[1], send_sem=send_sem.at[1],
            recv_sem=recv_sem.at[1], device_id=(me, sp + 1), device_id_type=MESH,
        )
        down_recv.wait_recv()

    @pl.when(has_lo)
    def _():
        down.wait_send()
        up_recv = pltpu.make_async_remote_copy(
            src_ref=send_buf.at[0], dst_ref=recv_buf.at[0], send_sem=send_sem.at[0],
            recv_sem=recv_sem.at[0], device_id=(me, sp - 1), device_id_type=MESH,
        )
        up_recv.wait_recv()

    below = jnp.where(has_lo, recv_buf[0], 0.0)
    above = jnp.where(has_hi, recv_buf[1], 0.0)
    acc[0] = [v + below[:, y * row:(y + 1) * row] for y, v in enumerate(acc[0])]
    acc[depth - 1] = [v + above[:, y * row:(y + 1) * row] for y, v in enumerate(acc[depth - 1])]
    pooled = []
    for zp in range(depth // 2):
        zmax = [jnp.maximum(u, v) for u, v in zip(acc[2 * zp], acc[2 * zp + 1])]
        for yp in range(heights // 2):
            pooled.append(jnp.maximum(zmax[2 * yp], zmax[2 * yp + 1]))
    m = jnp.concatenate(pooled, axis=1)
    m = jnp.maximum(m, pltpu.roll(m, m.shape[1] - 1, 1))
    brow = jnp.broadcast_to(b_ref[...].astype(jnp.float32), (filters, filters))
    r16 = lax.broadcasted_iota(jnp.int32, (filters, filters), 0)
    c16 = lax.broadcasted_iota(jnp.int32, (filters, filters), 1)
    bias = jnp.sum(jnp.where(r16 == c16, brow, 0.0), axis=1, keepdims=True)
    v = m + bias
    v = jnp.where(v > 0, v, slope * v).astype(jnp.bfloat16)
    r = lax.broadcasted_iota(jnp.int32, (m.shape[1], m.shape[1] // 2), 0)
    c = lax.broadcasted_iota(jnp.int32, (m.shape[1], m.shape[1] // 2), 1)
    pick = (r == 2 * c).astype(jnp.bfloat16)
    picked = jnp.dot(v, pick, preferred_element_type=jnp.float32).astype(o_ref.dtype)
    half = row // 2
    for zp in range(o_ref.shape[1]):
        for yp in range(o_ref.shape[2]):
            k = zp * o_ref.shape[2] + yp
            o_ref[:, zp, yp, :] = picked[:, k * half:(k + 1) * half]


def conv_pool(gathered, kernel, filter_bias, depth, height, across):
    filters = kernel.shape[0]
    weights = kernel.transpose(1, 2, 3, 0, 4)
    bias = filter_bias.reshape(1, filters)
    plane = height * across
    return pl.pallas_call(
        functools.partial(conv_kernel, plane=plane, row=across, depth=depth,
                          slabs=lax.axis_size("space")),
        out_shape=jax.ShapeDtypeStruct((filters, depth // 2, height // 2, across // 2), jnp.bfloat16),
        in_specs=[pl.BlockSpec(memory_space=pltpu.VMEM)] * 3,
        out_specs=pl.BlockSpec(memory_space=pltpu.VMEM),
        scratch_shapes=[
            pltpu.VMEM((2, filters, plane), jnp.float32),
            pltpu.VMEM((2, filters, plane), jnp.float32),
            pltpu.SemaphoreType.DMA((2,)),
            pltpu.SemaphoreType.DMA((2,)),
        ],
        compiler_params=pltpu.CompilerParams(collective_id=1, has_side_effects=True),
    )(gathered, weights, bias)


def on_device(volume, kernel, filter_bias):
    local_in, depth, height, across = volume.shape
    gathered = gather_filt(volume)
    return conv_pool(gathered, kernel, filter_bias, depth, height, across)


def solution(mesh):
    in_specs = (P("filt", "space", None, None), P("filt", None, None, None, None), P("filt"))
    out_specs = P("filt", "space", None, None)
    return jax.shard_map(
        on_device, mesh=mesh, in_specs=in_specs, out_specs=out_specs, check_vma=False
    )
```

time: 34.5 us -> 35.1 us (1.017)
  the two profiles are of different devices: /device:TPU:7 before, /device:TPU:32 now
where the time goes in v7:
time: 35.1 us; the launch traced here: 34.9 us
  Pallas kernels  33.6 us (96%)
  local copies, waits for them, and re-layouts  1.34 us (4%)
    pallas_call x1, Pallas kernels, gather_filt(): pl.pallas_call(functools.partial(gather_kernel, n), out_shape=jax.ShapeDt...  24.2 us
    pallas_call x1, Pallas kernels, conv_pool(): pl.pallas_call(functools.partial(conv_kernel, plane=plane, row=across, de...  9.39 us
    unnamed x1, local copies, waits for them, and re-layouts  1.34 us

profile of v7, /device:TPU:32, one launch (start us, length us, event | category | flops | bytes accessed | tf_op | source)
XLA Modules:
  0.0 34.9 jit_solution(18011288221300463225)
XLA Ops:
  0.0 24.2 %shard_map.37.g_ref = bf16[256,2048]{1,0:T(8,128)(2,1)} custom-call(bf16[8,4,4,128]{3,2,1,0:T(4,128)(2,1)} %v_ref.1), custom_call_target="tpu_custom_call" | custom-call | tf_op jit(solution)/shard_map/pallas_call | solution.py:96
  24.2 9.4 %shard_map.38 = bf16[16,2,2,64]{3,2,1,0:T(2,128)(2,1)} custom-call(bf16[256,2048]{1,0:T(8,128)(2,1)} %shard_map.37.g_ref, bf16[3,3,3,16,256]{4,3,2,1,0:T(8,128)(2,1)} %bitcast.2, bf16[1,16]{1,0:T(2,128)(2,1)} %bitcast.3), custom_call_target="tpu_custom_call" | custom-call | tf_op jit(solution)/shard_map/pallas_call | solution.py:245
  33.6 1.3 %copy.5 = bf16[16,2,2,64]{3,2,1,0:T(2,128)(2,1)} copy(bf16[16,2,2,64]{3,2,1,0:T(2,128)(2,1)} %shard_map.38) | data formatting | bytes 16384

commit v8 on v7

--- a/solution.py
+++ b/solution.py
@@ -116,6 +116,16 @@
     me = lax.axis_index("filt")
     has_lo = sp > 0
     has_hi = sp < slabs - 1
+    barrier = pltpu.get_barrier_semaphore()
+
+    @pl.when(has_lo)
+    def _():
+        pl.semaphore_signal(barrier, inc=1, device_id=(me, sp - 1), device_id_type=MESH)
+
+    @pl.when(has_hi)
+    def _():
+        pl.semaphore_signal(barrier, inc=1, device_id=(me, sp + 1), device_id_type=MESH)
+
     g = g_ref[...]
     cols = g.shape[1]
     heights = plane // row
@@ -129,12 +139,22 @@
          for a in range(3) for b in range(3)],
         axis=0,
     )
-    q = jnp.dot(weights, stacked, preferred_element_type=jnp.float32)
     filters = w_ref.shape[3]
+    taps = 3 * filters
+    edge_q = {
+        (0, depth - 1): jnp.dot(weights[:taps], stacked[:, (depth - 1) * plane:],
+                                preferred_element_type=jnp.float32),
+        (2, 0): jnp.dot(weights[2 * taps:], stacked[:, :plane],
+                        preferred_element_type=jnp.float32),
+    }
+    q = None
 
     def tap_row(a, b, p, y):
         if not 0 <= y < heights:
             return None
+        if q is None:
+            t = b * filters
+            return edge_q[(a, p)][t:t + filters, y * row:(y + 1) * row]
         t = (a * 3 + b) * filters
         c0 = p * plane + y * row
         return q[t:t + filters, c0:c0 + row]
@@ -152,16 +172,6 @@
 
     send_buf[0] = jnp.concatenate(plane_sum(0, depth - 1), axis=1)
     send_buf[1] = jnp.concatenate(plane_sum(2, 0), axis=1)
-    barrier = pltpu.get_barrier_semaphore()
-
-    @pl.when(has_lo)
-    def _():
-        pl.semaphore_signal(barrier, inc=1, device_id=(me, sp - 1), device_id_type=MESH)
-
-    @pl.when(has_hi)
-    def _():
-        pl.semaphore_signal(barrier, inc=1, device_id=(me, sp + 1), device_id_type=MESH)
-
     pl.semaphore_wait(barrier, has_lo.astype(jnp.int32) + has_hi.astype(jnp.int32))
     up = pltpu.make_async_remote_copy(
         src_ref=send_buf.at[0], dst_ref=recv_buf.at[0], send_sem=send_sem.at[0],
@@ -180,6 +190,7 @@
     def _():
         down.start()
 
+    q = jnp.dot(weights, stacked, preferred_element_type=jnp.float32)
     acc = []
     for z in range(depth):
         rows_z = None

time: 35.1 us -> 34.8 us (level)
  Pallas kernels: 33.6 us -> 33.2 us
    pallas_call x1, Pallas kernels: 9.39 us -> 9.01 us  [conv_pool(): pl.pallas_call(functools.partial(conv_kernel, plane=plane, row=across, de...]
where the time goes in v8:
time: 34.8 us; the launch traced here: 34.5 us
  Pallas kernels  33.2 us (95%)
  local copies, waits for them, and re-layouts  1.34 us (4%)
    pallas_call x1, Pallas kernels, gather_filt(): pl.pallas_call(functools.partial(gather_kernel, n), out_shape=jax.ShapeDt...  24.2 us
    pallas_call x1, Pallas kernels, conv_pool(): pl.pallas_call(functools.partial(conv_kernel, plane=plane, row=across, de...  9.01 us
    unnamed x1, local copies, waits for them, and re-layouts  1.34 us

profile of v8, /device:TPU:32, one launch (start us, length us, event | category | flops | bytes accessed | tf_op | source)
XLA Modules:
  0.0 34.5 jit_solution(11078049273308639628)
XLA Ops:
  0.0 24.2 %shard_map.37.g_ref = bf16[256,2048]{1,0:T(8,128)(2,1)} custom-call(bf16[8,4,4,128]{3,2,1,0:T(4,128)(2,1)} %v_ref.1), custom_call_target="tpu_custom_call" | custom-call | tf_op jit(solution)/shard_map/pallas_call | solution.py:96
  24.2 9.0 %shard_map.38 = bf16[16,2,2,64]{3,2,1,0:T(2,128)(2,1)} custom-call(bf16[256,2048]{1,0:T(8,128)(2,1)} %shard_map.37.g_ref, bf16[3,3,3,16,256]{4,3,2,1,0:T(8,128)(2,1)} %bitcast.2, bf16[1,16]{1,0:T(2,128)(2,1)} %bitcast.3), custom_call_target="tpu_custom_call" | custom-call | tf_op jit(solution)/shard_map/pallas_call | solution.py:256
  33.2 1.3 %copy.5 = bf16[16,2,2,64]{3,2,1,0:T(2,128)(2,1)} copy(bf16[16,2,2,64]{3,2,1,0:T(2,128)(2,1)} %shard_map.38) | data formatting | bytes 16384

commit v9 on v7

--- a/solution.py
+++ b/solution.py
@@ -11,7 +11,9 @@
 MESH = pl.DeviceIdType.MESH
 
 
-def gather_kernel(n, v_ref, out_ref, x_ref, local_sem, send_sem, fwd_sem, relay_sem, recv_sem):
+def gather_kernel(n, slabs, v_ref, w_ref, out_ref, part_ref, x_ref, edge_in, send_buf,
+                  recv_buf, local_sem, send_sem, fwd_sem, relay_sem, recv_sem, edge_sem,
+                  part_send, part_recv):
     depth, height, across = v_ref.shape[1:]
     for z in range(depth):
         for y in range(height):
@@ -45,7 +47,20 @@
     barrier = pltpu.get_barrier_semaphore()
     for peer in [sib] + peers:
         pl.semaphore_signal(barrier, inc=1, device_id=(peer, sp), device_id_type=MESH)
-    pl.semaphore_wait(barrier, 1 + len(peers))
+    has_lo = sp > 0
+    has_hi = sp < slabs - 1
+
+    @pl.when(has_lo)
+    def _():
+        pl.semaphore_signal(barrier, inc=1, device_id=(me, sp - 1), device_id_type=MESH)
+
+    @pl.when(has_hi)
+    def _():
+        pl.semaphore_signal(barrier, inc=1, device_id=(me, sp + 1), device_id_type=MESH)
+
+    pl.semaphore_wait(
+        barrier, 1 + len(peers) + has_lo.astype(jnp.int32) + has_hi.astype(jnp.int32)
+    )
 
     def copy(src, dst, sem, recv, dev_id):
         return pltpu.make_async_remote_copy(
@@ -83,39 +98,112 @@
     for k in range(chips):
         src = (sources[k - 1] if k else me) + 1 - 2 * core
         main_copy(main_at(src), src, fwd_sem.at[0, 0], sib).wait_recv()
+    local.wait()
+    edges = []
+    for k, p in enumerate((depth - 1, 0)):
+        e = pltpu.make_async_copy(out_ref.at[:, pl.ds(p * plane, plane)], edge_in.at[k],
+                                  edge_sem.at[k])
+        e.start()
+        edges.append(e)
+    filters = w_ref.shape[3]
+    for k, a in enumerate((0, 2)):
+        edges[k].wait()
+        g = edge_in[k]
+        x = lax.broadcasted_iota(jnp.int32, g.shape, 1) % across
+        zero = jnp.zeros_like(g)
+        left = jnp.where(x == 0, zero, pltpu.roll(g, 1, 1))
+        right = jnp.where(x == across - 1, zero, pltpu.roll(g, plane - 1, 1))
+        stacked = jnp.concatenate([left, g, right], axis=0)
+        weights = jnp.concatenate(
+            [jnp.concatenate([w_ref[a, b, c] for c in range(3)], axis=1) for b in range(3)],
+            axis=0,
+        )
+        q = jnp.dot(weights, stacked, preferred_element_type=jnp.float32)
+        tiles = []
+        for y in range(height):
+            total = None
+            for b in range(3):
+                yi = y + b - 1
+                if 0 <= yi < height:
+                    v = q[b * filters:(b + 1) * filters, yi * across:(yi + 1) * across]
+                    total = v if total is None else total + v
+            tiles.append(total)
+        send_buf[k] = jnp.concatenate(tiles, axis=1)
+    up = pltpu.make_async_remote_copy(
+        src_ref=send_buf.at[0], dst_ref=recv_buf.at[0], send_sem=part_send.at[0],
+        recv_sem=part_recv.at[0], device_id=(me, sp + 1), device_id_type=MESH,
+    )
+    down = pltpu.make_async_remote_copy(
+        src_ref=send_buf.at[1], dst_ref=recv_buf.at[1], send_sem=part_send.at[1],
+        recv_sem=part_recv.at[1], device_id=(me, sp - 1), device_id_type=MESH,
+    )
+
+    @pl.when(has_hi)
+    def _():
+        up.start()
+
+    @pl.when(has_lo)
+    def _():
+        down.start()
+
     for c in sends + forwards + relays:
         c.wait_send()
-    local.wait()
-
-
-def gather_filt(block):
+
+    @pl.when(has_hi)
+    def _():
+        up.wait_send()
+        pltpu.make_async_remote_copy(
+            src_ref=send_buf.at[1], dst_ref=recv_buf.at[1], send_sem=part_send.at[1],
+            recv_sem=part_recv.at[1], device_id=(me, sp + 1), device_id_type=MESH,
+        ).wait_recv()
+
+    @pl.when(has_lo)
+    def _():
+        down.wait_send()
+        pltpu.make_async_remote_copy(
+            src_ref=send_buf.at[0], dst_ref=recv_buf.at[0], send_sem=part_send.at[0],
+            recv_sem=part_recv.at[0], device_id=(me, sp - 1), device_id_type=MESH,
+        ).wait_recv()
+
+    part_ref[0] = jnp.where(has_lo, recv_buf[0], 0.0)
+    part_ref[1] = jnp.where(has_hi, recv_buf[1], 0.0)
+
+
+def gather_filt(block, weights):
     n = lax.axis_size("filt")
+    slabs = lax.axis_size("space")
     rows = block.shape[0]
     cols = block.size // rows
+    plane = cols // block.shape[1]
+    filters = weights.shape[3]
     chips = n // 2
     return pl.pallas_call(
-        functools.partial(gather_kernel, n),
-        out_shape=jax.ShapeDtypeStruct((n * rows, cols), block.dtype),
-        in_specs=[pl.BlockSpec(memory_space=pltpu.VMEM)],
-        out_specs=pl.BlockSpec(memory_space=pl.ANY),
+        functools.partial(gather_kernel, n, slabs),
+        out_shape=(
+            jax.ShapeDtypeStruct((n * rows, cols), block.dtype),
+            jax.ShapeDtypeStruct((2, filters, plane), jnp.float32),
+        ),
+        in_specs=[pl.BlockSpec(memory_space=pltpu.VMEM)] * 2,
+        out_specs=(pl.BlockSpec(memory_space=pl.ANY), pl.BlockSpec(memory_space=pltpu.VMEM)),
         scratch_shapes=[
             pltpu.VMEM((rows, cols), block.dtype),
+            pltpu.VMEM((2, n * rows, plane), block.dtype),
+            pltpu.VMEM((2, filters, plane), jnp.float32),
+            pltpu.VMEM((2, filters, plane), jnp.float32),
             pltpu.SemaphoreType.DMA((1,)),
             pltpu.SemaphoreType.DMA((chips,)),
             pltpu.SemaphoreType.DMA((1, chips)),
             pltpu.SemaphoreType.DMA((2, chips // 4)),
             pltpu.SemaphoreType.DMA((n,)),
+            pltpu.SemaphoreType.DMA((2,)),
+            pltpu.SemaphoreType.DMA((2,)),
+            pltpu.SemaphoreType.DMA((2,)),
         ],
         compiler_params=pltpu.CompilerParams(collective_id=0, has_side_effects=True),
-    )(block)
-
-
-def conv_kernel(g_ref, w_ref, b_ref, o_ref, send_buf, recv_buf, send_sem, recv_sem, *,
-                plane, row, depth, slabs):
-    sp = lax.axis_index("space")
-    me = lax.axis_index("filt")
-    has_lo = sp > 0
-    has_hi = sp < slabs - 1
+    )(block, weights)
+
+
+def conv_kernel(g_ref, w_ref, b_ref, p_ref, o_ref, *, plane, row, depth):
     g = g_ref[...]
     cols = g.shape[1]
     heights = plane // row
@@ -129,8 +217,8 @@
          for a in range(3) for b in range(3)],
         axis=0,
     )
+    filters = w_ref.shape[3]
     q = jnp.dot(weights, stacked, preferred_element_type=jnp.float32)
-    filters = w_ref.shape[3]
 
     def tap_row(a, b, p, y):
         if not 0 <= y < heights:
@@ -150,36 +238,6 @@
             out.append(total)
         return out
 
-    send_buf[0] = jnp.concatenate(plane_sum(0, depth - 1), axis=1)
-    send_buf[1] = jnp.concatenate(plane_sum(2, 0), axis=1)
-    barrier = pltpu.get_barrier_semaphore()
-
-    @pl.when(has_lo)
-    def _():
-        pl.semaphore_signal(barrier, inc=1, device_id=(me, sp - 1), device_id_type=MESH)
-
-    @pl.when(has_hi)
-    def _():
-        pl.semaphore_signal(barrier, inc=1, device_id=(me, sp + 1), device_id_type=MESH)
-
-    pl.semaphore_wait(barrier, has_lo.astype(jnp.int32) + has_hi.astype(jnp.int32))
-    up = pltpu.make_async_remote_copy(
-        src_ref=send_buf.at[0], dst_ref=recv_buf.at[0], send_sem=send_sem.at[0],
-        recv_sem=recv_sem.at[0], device_id=(me, sp + 1), device_id_type=MESH,
-    )
-    down = pltpu.make_async_remote_copy(
-        src_ref=send_buf.at[1], dst_ref=recv_buf.at[1], send_sem=send_sem.at[1],
-        recv_sem=recv_sem.at[1], device_id=(me, sp - 1), device_id_type=MESH,
-    )
-
-    @pl.when(has_hi)
-    def _():
-        up.start()
-
-    @pl.when(has_lo)
-    def _():
-        down.start()
-
     acc = []
     for z in range(depth):
         rows_z = None
@@ -191,26 +249,8 @@
             rows_z = part if rows_z is None else [u + v for u, v in zip(rows_z, part)]
         acc.append(rows_z)
 
-    @pl.when(has_hi)
-    def _():
-        up.wait_send()
-        down_recv = pltpu.make_async_remote_copy(
-            src_ref=send_buf.at[1], dst_ref=recv_buf.at[1], send_sem=send_sem.at[1],
-            recv_sem=recv_sem.at[1], device_id=(me, sp + 1), device_id_type=MESH,
-        )
-        down_recv.wait_recv()
-
-    @pl.when(has_lo)
-    def _():
-        down.wait_send()
-        up_recv = pltpu.make_async_remote_copy(
-            src_ref=send_buf.at[0], dst_ref=recv_buf.at[0], send_sem=send_sem.at[0],
-            recv_sem=recv_sem.at[0], device_id=(me, sp - 1), device_id_type=MESH,
-        )
-        up_recv.wait_recv()
-
-    below = jnp.where(has_lo, recv_buf[0], 0.0)
-    above = jnp.where(has_hi, recv_buf[1], 0.0)
+    below = p_ref[0]
+    above = p_ref[1]
     acc[0] = [v + below[:, y * row:(y + 1) * row] for y, v in enumerate(acc[0])]
     acc[depth - 1] = [v + above[:, y * row:(y + 1) * row] for y, v in enumerate(acc[depth - 1])]
     pooled = []
@@ -237,31 +277,23 @@
             o_ref[:, zp, yp, :] = picked[:, k * half:(k + 1) * half]
 
 
-def conv_pool(gathered, kernel, filter_bias, depth, height, across):
-    filters = kernel.shape[0]
-    weights = kernel.transpose(1, 2, 3, 0, 4)
+def conv_pool(gathered, parts, weights, filter_bias, depth, height, across):
+    filters = weights.shape[3]
     bias = filter_bias.reshape(1, filters)
     plane = height * across
     return pl.pallas_call(
-        functools.partial(conv_kernel, plane=plane, row=across, depth=depth,
-                          slabs=lax.axis_size("space")),
+        functools.partial(conv_kernel, plane=plane, row=across, depth=depth),
         out_shape=jax.ShapeDtypeStruct((filters, depth // 2, height // 2, across // 2), jnp.bfloat16),
-        in_specs=[pl.BlockSpec(memory_space=pltpu.VMEM)] * 3,
+        in_specs=[pl.BlockSpec(memory_space=pltpu.VMEM)] * 4,
         out_specs=pl.BlockSpec(memory_space=pltpu.VMEM),
-        scratch_shapes=[
-            pltpu.VMEM((2, filters, plane), jnp.float32),
-            pltpu.VMEM((2, filters, plane), jnp.float32),
-            pltpu.SemaphoreType.DMA((2,)),
-            pltpu.SemaphoreType.DMA((2,)),
-        ],
-        compiler_params=pltpu.CompilerParams(collective_id=1, has_side_effects=True),
-    )(gathered, weights, bias)
+    )(gathered, weights, bias, parts)
 
 
 def on_device(volume, kernel, filter_bias):
     local_in, depth, height, across = volume.shape
-    gathered = gather_filt(volume)
-    return conv_pool(gathered, kernel, filter_bias, depth, height, across)
+    weights = kernel.transpose(1, 2, 3, 0, 4)
+    gathered, parts = gather_filt(volume, weights)
+    return conv_pool(gathered, parts, weights, filter_bias, depth, height, across)
 
 
 def solution(mesh):

time: 35.1 us -> 33.4 us (0.952)
  the two profiles are of different devices: /device:TPU:32 before, /device:TPU:7 now
where the time goes in v9:
time: 33.4 us; the launch traced here: 32.9 us
  Pallas kernels  32.9 us (99%)
    pallas_call x1, Pallas kernels, gather_filt(): pl.pallas_call(functools.partial(gather_kernel, n, slabs), out_shape=(jax...  29.8 us
    pallas_call x1, Pallas kernels, conv_pool(): pl.pallas_call(functools.partial(conv_kernel, plane=plane, row=across, de...  3.17 us

profile of v9, /device:TPU:7, one launch (start us, length us, event | category | flops | bytes accessed | tf_op | source)
XLA Modules:
  0.0 32.9 jit_solution(3196919743624795131)
XLA Ops:
  0.0 29.8 %shard_map.37 = (bf16[256,2048]{1,0:T(8,128)(2,1)}, f32[2,16,512]{2,1,0:T(8,128)}) custom-call(bf16[8,4,4,128]{3,2,1,0:T(4,128)(2,1)} %v_ref.1, bf16[3,3,3,16,256]{4,3,2,1,0:T(8,128)(2,1)} %bitcast.2), custom_call_target="tpu_custom_call" | custom-call | tf_op jit(solution)/shard_map/pallas_call | solution.py:180
  29.8 3.2 %shard_map.38 = bf16[16,2,2,64]{3,2,1,0:T(2,128)(2,1)} custom-call(bf16[256,2048]{1,0:T(8,128)(2,1)} %get-tuple-element.7.g_ref, bf16[3,3,3,16,256]{4,3,2,1,0:T(8,128)(2,1)} %bitcast.3, bf16[1,16]{1,0:T(2,128)(2,1)} %bitcast.4, f32[2,16,512]{2,1,0:T(8,128)} %get-tuple-element.8.p_ref), custom_call_target="tpu_custom_call" | custom-call | tf_op jit(solution)/shard_map/pallas_call | solution.py:284

commit v10 on v9

--- a/solution.py
+++ b/solution.py
@@ -11,8 +11,8 @@
 MESH = pl.DeviceIdType.MESH
 
 
-def gather_kernel(n, slabs, v_ref, w_ref, out_ref, part_ref, x_ref, edge_in, send_buf,
-                  recv_buf, local_sem, send_sem, fwd_sem, relay_sem, recv_sem, edge_sem,
+def gather_kernel(n, slabs, v_ref, w_ref, acc_ref, part_ref, out_ref, x_ref, send_buf,
+                  recv_buf, local_sem, send_sem, fwd_sem, relay_sem, recv_sem,
                   part_send, part_recv):
     depth, height, across = v_ref.shape[1:]
     for z in range(depth):
@@ -99,16 +99,9 @@
         src = (sources[k - 1] if k else me) + 1 - 2 * core
         main_copy(main_at(src), src, fwd_sem.at[0, 0], sib).wait_recv()
     local.wait()
-    edges = []
-    for k, p in enumerate((depth - 1, 0)):
-        e = pltpu.make_async_copy(out_ref.at[:, pl.ds(p * plane, plane)], edge_in.at[k],
-                                  edge_sem.at[k])
-        e.start()
-        edges.append(e)
     filters = w_ref.shape[3]
-    for k, a in enumerate((0, 2)):
-        edges[k].wait()
-        g = edge_in[k]
+    for k, (a, p) in enumerate(((0, depth - 1), (2, 0))):
+        g = out_ref[:, pl.ds(p * plane, plane)]
         x = lax.broadcasted_iota(jnp.int32, g.shape, 1) % across
         zero = jnp.zeros_like(g)
         left = jnp.where(x == 0, zero, pltpu.roll(g, 1, 1))
@@ -146,6 +139,7 @@
     def _():
         down.start()
 
+    acc_ref[...] = interior_conv(out_ref, w_ref, plane=plane, row=across, depth=depth)
     for c in sends + forwards + relays:
         c.wait_send()
 
@@ -180,14 +174,14 @@
     return pl.pallas_call(
         functools.partial(gather_kernel, n, slabs),
         out_shape=(
-            jax.ShapeDtypeStruct((n * rows, cols), block.dtype),
+            jax.ShapeDtypeStruct((filters, cols), jnp.float32),
             jax.ShapeDtypeStruct((2, filters, plane), jnp.float32),
         ),
         in_specs=[pl.BlockSpec(memory_space=pltpu.VMEM)] * 2,
-        out_specs=(pl.BlockSpec(memory_space=pl.ANY), pl.BlockSpec(memory_space=pltpu.VMEM)),
+        out_specs=(pl.BlockSpec(memory_space=pltpu.VMEM), pl.BlockSpec(memory_space=pltpu.VMEM)),
         scratch_shapes=[
+            pltpu.VMEM((n * rows, cols), block.dtype),
             pltpu.VMEM((rows, cols), block.dtype),
-            pltpu.VMEM((2, n * rows, plane), block.dtype),
             pltpu.VMEM((2, filters, plane), jnp.float32),
             pltpu.VMEM((2, filters, plane), jnp.float32),
             pltpu.SemaphoreType.DMA((1,)),
@@ -197,13 +191,12 @@
             pltpu.SemaphoreType.DMA((n,)),
             pltpu.SemaphoreType.DMA((2,)),
             pltpu.SemaphoreType.DMA((2,)),
-            pltpu.SemaphoreType.DMA((2,)),
         ],
         compiler_params=pltpu.CompilerParams(collective_id=0, has_side_effects=True),
     )(block, weights)
 
 
-def conv_kernel(g_ref, w_ref, b_ref, p_ref, o_ref, *, plane, row, depth):
+def interior_conv(g_ref, w_ref, *, plane, row, depth):
     g = g_ref[...]
     cols = g.shape[1]
     heights = plane // row
@@ -227,28 +220,27 @@
         c0 = p * plane + y * row
         return q[t:t + filters, c0:c0 + row]
 
-    def plane_sum(a, p):
-        out = []
+    tiles = []
+    for z in range(depth):
         for y in range(heights):
-            parts = [tap_row(a, b, p, y + b - 1) for b in range(3)]
-            parts = [v for v in parts if v is not None]
-            total = parts[0]
-            for v in parts[1:]:
-                total = total + v
-            out.append(total)
-        return out
-
-    acc = []
-    for z in range(depth):
-        rows_z = None
-        for a in range(3):
-            p = z + a - 1
-            if not 0 <= p < depth:
-                continue
-            part = plane_sum(a, p)
-            rows_z = part if rows_z is None else [u + v for u, v in zip(rows_z, part)]
-        acc.append(rows_z)
-
+            total = None
+            for a in range(3):
+                p = z + a - 1
+                if not 0 <= p < depth:
+                    continue
+                for b in range(3):
+                    v = tap_row(a, b, p, y + b - 1)
+                    if v is not None:
+                        total = v if total is None else total + v
+            tiles.append(total)
+    return jnp.concatenate(tiles, axis=1)
+
+
+def finish_kernel(acc_ref, p_ref, b_ref, o_ref, *, plane, row, depth):
+    filters = acc_ref.shape[0]
+    heights = plane // row
+    acc = [[acc_ref[:, pl.ds((z * heights + y) * row, row)] for y in range(heights)]
+           for z in range(depth)]
     below = p_ref[0]
     above = p_ref[1]
     acc[0] = [v + below[:, y * row:(y + 1) * row] for y, v in enumerate(acc[0])]
@@ -277,23 +269,17 @@
             o_ref[:, zp, yp, :] = picked[:, k * half:(k + 1) * half]
 
 
-def conv_pool(gathered, parts, weights, filter_bias, depth, height, across):
-    filters = weights.shape[3]
-    bias = filter_bias.reshape(1, filters)
-    plane = height * across
-    return pl.pallas_call(
-        functools.partial(conv_kernel, plane=plane, row=across, depth=depth),
-        out_shape=jax.ShapeDtypeStruct((filters, depth // 2, height // 2, across // 2), jnp.bfloat16),
-        in_specs=[pl.BlockSpec(memory_space=pltpu.VMEM)] * 4,
-        out_specs=pl.BlockSpec(memory_space=pltpu.VMEM),
-    )(gathered, weights, bias, parts)
-
-
 def on_device(volume, kernel, filter_bias):
     local_in, depth, height, across = volume.shape
     weights = kernel.transpose(1, 2, 3, 0, 4)
-    gathered, parts = gather_filt(volume, weights)
-    return conv_pool(gathered, parts, weights, filter_bias, depth, height, across)
+    acc, parts = gather_filt(volume, weights)
+    filters = weights.shape[3]
+    return pl.pallas_call(
+        functools.partial(finish_kernel, plane=height * across, row=across, depth=depth),
+        out_shape=jax.ShapeDtypeStruct((filters, depth // 2, height // 2, across // 2), jnp.bfloat16),
+        in_specs=[pl.BlockSpec(memory_space=pltpu.VMEM)] * 3,
+        out_specs=pl.BlockSpec(memory_space=pltpu.VMEM),
+    )(acc, parts, filter_bias.reshape(1, filters))
 
 
 def solution(mesh):

time: 33.4 us -> 30.3 us (0.907)
  Pallas kernels: 32.9 us -> 29.7 us
    pallas_call x1, Pallas kernels: 29.8 us -> 27.9 us  [gather_filt(): pl.pallas_call(functools.partial(gather_kernel, n, slabs), out_shape=(jax...]
    pallas_call x1, Pallas kernels: 3.17 us -> 1.86 us  [on_device(): pl.pallas_call(functools.partial(finish_kernel, plane=height * across, ro...]
where the time goes in v10:
time: 30.3 us; the launch traced here: 29.8 us
  Pallas kernels  29.7 us (98%)
    pallas_call x1, Pallas kernels, gather_filt(): pl.pallas_call(functools.partial(gather_kernel, n, slabs), out_shape=(jax...  27.9 us
    pallas_call x1, Pallas kernels, on_device(): pl.pallas_call(functools.partial(finish_kernel, plane=height * across, ro...  1.86 us

profile of v10, /device:TPU:7, one launch (start us, length us, event | category | flops | bytes accessed | tf_op | source)
XLA Modules:
  0.0 29.8 jit_solution(1250239744180536771)
XLA Ops:
  0.0 27.9 %shard_map.37 = (f32[16,2048]{1,0:T(8,128)}, f32[2,16,512]{2,1,0:T(8,128)}) custom-call(bf16[8,4,4,128]{3,2,1,0:T(4,128)(2,1)} %v_ref.1, bf16[3,3,3,16,256]{4,3,2,1,0:T(8,128)(2,1)} %bitcast.2), custom_call_target="tpu_custom_call" | custom-call | tf_op jit(solution)/shard_map/pallas_call | solution.py:174
  27.9 1.9 %shard_map.38 = bf16[16,2,2,64]{3,2,1,0:T(2,128)(2,1)} custom-call(f32[16,2048]{1,0:T(8,128)} %get-tuple-element.7.acc_ref, f32[2,16,512]{2,1,0:T(8,128)} %get-tuple-element.8.p_ref, bf16[1,16]{1,0:T(2,128)(2,1)} %bitcast.3), custom_call_target="tpu_custom_call" | custom-call | tf_op jit(solution)/shard_map/pallas_call | solution.py:277

commit v11 on v10

--- a/solution.py
+++ b/solution.py
@@ -13,7 +13,7 @@
 
 def gather_kernel(n, slabs, v_ref, w_ref, acc_ref, part_ref, out_ref, x_ref, send_buf,
                   recv_buf, local_sem, send_sem, fwd_sem, relay_sem, recv_sem,
-                  part_send, part_recv):
+                  part_send, part_recv, half_recv, send2_sem):
     depth, height, across = v_ref.shape[1:]
     for z in range(depth):
         for y in range(height):
@@ -74,24 +74,44 @@
     local = pltpu.make_async_copy(x_ref, main_at(me), local_sem.at[0])
     local.start()
     sends = [main_copy(x_ref, me, send_sem.at[0], sib)]
-    for k, peer in enumerate(peers):
-        sends.append(main_copy(x_ref, me, send_sem.at[k + 1], peer))
+    later = []
+    for k, ((dy, dz), peer) in enumerate(zip(direct, peers)):
+        if dz in (1, 3):
+            first = pl.ds(0 if dz == 1 else half, half)
+            rest = pl.ds(half if dz == 1 else 0, half)
+            dst = out_ref.at[rows_of(me), first]
+            sends.append(copy(x_ref.at[:, first], dst, send_sem.at[k + 1], half_recv.at[me],
+                              (peer, sp)))
+            dst = out_ref.at[rows_of(me), rest]
+            later.append(copy(x_ref.at[:, rest], dst, send2_sem.at[k], recv_sem.at[me],
+                              (peer, sp)))
+        else:
+            later.append(main_copy(x_ref, me, send_sem.at[k + 1], peer))
+    sends += later
     for c in sends:
         c.start()
     forwards = []
     relays = []
     sources = []
-    for k, (dy, dz) in enumerate(direct + far):
-        src = dev(-dy, -dz)
-        sources.append(src)
-        main_copy(main_at(src), src, fwd_sem.at[0, k], src).wait_recv()
+    for dy, dz in direct:
         if dz in (1, 3):
+            src = dev(-dy, -dz)
             part = pl.ds(0 if dz == 1 else half, half)
             held = out_ref.at[rows_of(src), part]
+            copy(held, held, relay_sem.at[dz // 2, dy], half_recv.at[src], (src, sp)).wait_recv()
             target = dev(0, 1 if dz == 1 else -1)
             r = copy(held, held, relay_sem.at[dz // 2, dy], recv_sem.at[src], (target, sp))
             r.start()
             relays.append(r)
+    for k, (dy, dz) in enumerate(direct + far):
+        src = dev(-dy, -dz)
+        sources.append(src)
+        if dz in (1, 3):
+            rest = pl.ds(half if dz == 1 else 0, half)
+            held = out_ref.at[rows_of(src), rest]
+            copy(held, held, fwd_sem.at[0, k], recv_sem.at[src], (src, sp)).wait_recv()
+        else:
+            main_copy(main_at(src), src, fwd_sem.at[0, k], src).wait_recv()
         c = main_copy(main_at(src), src, fwd_sem.at[0, k], sib)
         c.start()
         forwards.append(c)
@@ -191,6 +211,8 @@
             pltpu.SemaphoreType.DMA((n,)),
             pltpu.SemaphoreType.DMA((2,)),
             pltpu.SemaphoreType.DMA((2,)),
+            pltpu.SemaphoreType.DMA((n,)),
+            pltpu.SemaphoreType.DMA((chips,)),
         ],
         compiler_params=pltpu.CompilerParams(collective_id=0, has_side_effects=True),
     )(block, weights)

time: 30.3 us -> 29.6 us (0.977)
  Pallas kernels: 29.7 us -> 29.2 us
    pallas_call x1, Pallas kernels: 27.9 us -> 27.4 us  [gather_filt(): pl.pallas_call(functools.partial(gather_kernel, n, slabs), out_shape=(jax...]
where the time goes in v11:
time: 29.6 us; the launch traced here: 29.2 us
  Pallas kernels  29.2 us (99%)
    pallas_call x1, Pallas kernels, gather_filt(): pl.pallas_call(functools.partial(gather_kernel, n, slabs), out_shape=(jax...  27.4 us
    pallas_call x1, Pallas kernels, on_device(): pl.pallas_call(functools.partial(finish_kernel, plane=height * across, ro...  1.86 us

profile of v11, /device:TPU:7, one launch (start us, length us, event | category | flops | bytes accessed | tf_op | source)
XLA Modules:
  0.0 29.2 jit_solution(5190879838307875699)
XLA Ops:
  0.0 27.4 %shard_map.37 = (f32[16,2048]{1,0:T(8,128)}, f32[2,16,512]{2,1,0:T(8,128)}) custom-call(bf16[8,4,4,128]{3,2,1,0:T(4,128)(2,1)} %v_ref.1, bf16[3,3,3,16,256]{4,3,2,1,0:T(8,128)(2,1)} %bitcast.2), custom_call_target="tpu_custom_call" | custom-call | tf_op jit(solution)/shard_map/pallas_call | solution.py:194
  27.4 1.9 %shard_map.38 = bf16[16,2,2,64]{3,2,1,0:T(2,128)(2,1)} custom-call(f32[16,2048]{1,0:T(8,128)} %get-tuple-element.7.acc_ref, f32[2,16,512]{2,1,0:T(8,128)} %get-tuple-element.8.p_ref, bf16[1,16]{1,0:T(2,128)(2,1)} %bitcast.3), custom_call_target="tpu_custom_call" | custom-call | tf_op jit(solution)/shard_map/pallas_call | solution.py:299

commit v12 on v11

--- a/solution.py
+++ b/solution.py
@@ -11,7 +11,7 @@
 MESH = pl.DeviceIdType.MESH
 
 
-def gather_kernel(n, slabs, v_ref, w_ref, acc_ref, part_ref, out_ref, x_ref, send_buf,
+def gather_kernel(n, slabs, v_ref, w_ref, b_ref, o_ref, acc_ref, part_ref, out_ref, x_ref, send_buf,
                   recv_buf, local_sem, send_sem, fwd_sem, relay_sem, recv_sem,
                   part_send, part_recv, half_recv, send2_sem):
     depth, height, across = v_ref.shape[1:]
@@ -181,25 +181,25 @@
 
     part_ref[0] = jnp.where(has_lo, recv_buf[0], 0.0)
     part_ref[1] = jnp.where(has_hi, recv_buf[1], 0.0)
-
-
-def gather_filt(block, weights):
+    finish_kernel(acc_ref, part_ref, b_ref, o_ref, plane=plane, row=across, depth=depth)
+
+
+def gather_filt(block, weights, bias):
     n = lax.axis_size("filt")
     slabs = lax.axis_size("space")
-    rows = block.shape[0]
+    rows, depth, height, across = block.shape
     cols = block.size // rows
-    plane = cols // block.shape[1]
+    plane = cols // depth
     filters = weights.shape[3]
     chips = n // 2
     return pl.pallas_call(
         functools.partial(gather_kernel, n, slabs),
-        out_shape=(
-            jax.ShapeDtypeStruct((filters, cols), jnp.float32),
-            jax.ShapeDtypeStruct((2, filters, plane), jnp.float32),
-        ),
-        in_specs=[pl.BlockSpec(memory_space=pltpu.VMEM)] * 2,
-        out_specs=(pl.BlockSpec(memory_space=pltpu.VMEM), pl.BlockSpec(memory_space=pltpu.VMEM)),
+        out_shape=jax.ShapeDtypeStruct((filters, depth // 2, height // 2, across // 2), jnp.bfloat16),
+        in_specs=[pl.BlockSpec(memory_space=pltpu.VMEM)] * 3,
+        out_specs=pl.BlockSpec(memory_space=pltpu.VMEM),
         scratch_shapes=[
+            pltpu.VMEM((filters, cols), jnp.float32),
+            pltpu.VMEM((2, filters, plane), jnp.float32),
             pltpu.VMEM((n * rows, cols), block.dtype),
             pltpu.VMEM((rows, cols), block.dtype),
             pltpu.VMEM((2, filters, plane), jnp.float32),
@@ -215,7 +215,7 @@
             pltpu.SemaphoreType.DMA((chips,)),
         ],
         compiler_params=pltpu.CompilerParams(collective_id=0, has_side_effects=True),
-    )(block, weights)
+    )(block, weights, bias)
 
 
 def interior_conv(g_ref, w_ref, *, plane, row, depth):
@@ -294,14 +294,7 @@
 def on_device(volume, kernel, filter_bias):
     local_in, depth, height, across = volume.shape
     weights = kernel.transpose(1, 2, 3, 0, 4)
-    acc, parts = gather_filt(volume, weights)
-    filters = weights.shape[3]
-    return pl.pallas_call(
-        functools.partial(finish_kernel, plane=height * across, row=across, depth=depth),
-        out_shape=jax.ShapeDtypeStruct((filters, depth // 2, height // 2, across // 2), jnp.bfloat16),
-        in_specs=[pl.BlockSpec(memory_space=pltpu.VMEM)] * 3,
-        out_specs=pl.BlockSpec(memory_space=pltpu.VMEM),
-    )(acc, parts, filter_bias.reshape(1, filters))
+    return gather_filt(volume, weights, filter_bias.reshape(1, -1))
 
 
 def solution(mesh):

time: 29.6 us -> 29.4 us (level)
  Pallas kernels: 29.2 us -> 27.6 us
  local copies, waits for them, and re-layouts: 0 us -> 1.34 us
    pallas_call x2 -> x1, Pallas kernels: 29.2 us -> 27.6 us  [gather_filt(): pl.pallas_call(functools.partial(gather_kernel, n, slabs), out_shape=jax....]
    unnamed x0 -> x1, local copies, waits for them, and re-layouts: none -> 1.34 us
where the time goes in v12:
time: 29.4 us; the launch traced here: 28.9 us
  Pallas kernels  27.6 us (94%)
  local copies, waits for them, and re-layouts  1.34 us (5%)
    pallas_call x1, Pallas kernels, gather_filt(): pl.pallas_call(functools.partial(gather_kernel, n, slabs), out_shape=jax....  27.6 us
    unnamed x1, local copies, waits for them, and re-layouts  1.34 us

profile of v12, /device:TPU:7, one launch (start us, length us, event | category | flops | bytes accessed | tf_op | source)
XLA Modules:
  0.0 28.9 jit_solution(3941474757706385846)
XLA Ops:
  0.0 27.6 %shard_map.37 = bf16[16,2,2,64]{3,2,1,0:T(2,128)(2,1)} custom-call(bf16[8,4,4,128]{3,2,1,0:T(4,128)(2,1)} %v_ref.1, bf16[3,3,3,16,256]{4,3,2,1,0:T(8,128)(2,1)} %bitcast.2, bf16[1,16]{1,0:T(2,128)(2,1)} %bitcast.3), custom_call_target="tpu_custom_call" | custom-call | tf_op jit(solution)/shard_map/pallas_call | solution.py:195
  27.6 1.3 %copy.5 = bf16[16,2,2,64]{3,2,1,0:T(2,128)(2,1)} copy(bf16[16,2,2,64]{3,2,1,0:T(2,128)(2,1)} %shard_map.37) | data formatting | bytes 16384

commit v13 on v12

--- a/solution.py
+++ b/solution.py
@@ -72,7 +72,6 @@
         return copy(src, main_at(slot), sem, recv_sem.at[slot], (dev_id, sp))
 
     local = pltpu.make_async_copy(x_ref, main_at(me), local_sem.at[0])
-    local.start()
     sends = [main_copy(x_ref, me, send_sem.at[0], sib)]
     later = []
     for k, ((dy, dz), peer) in enumerate(zip(direct, peers)):
@@ -87,9 +86,10 @@
                               (peer, sp)))
         else:
             later.append(main_copy(x_ref, me, send_sem.at[k + 1], peer))
-    sends += later
+    sends = sends[1:] + later + sends[:1]
     for c in sends:
         c.start()
+    local.start()
     forwards = []
     relays = []
     sources = []

time: 29.4 us -> 29.3 us (level)
  no operation moved by 1% of the time
where the time goes in v13:
time: 29.3 us; the launch traced here: 28.8 us
  Pallas kernels  27.5 us (94%)
  local copies, waits for them, and re-layouts  1.34 us (5%)
    pallas_call x1, Pallas kernels, gather_filt(): pl.pallas_call(functools.partial(gather_kernel, n, slabs), out_shape=jax....  27.5 us
    unnamed x1, local copies, waits for them, and re-layouts  1.34 us

profile of v13, /device:TPU:7, one launch (start us, length us, event | category | flops | bytes accessed | tf_op | source)
XLA Modules:
  0.0 28.8 jit_solution(16974033216182284049)
XLA Ops:
  0.0 27.5 %shard_map.37 = bf16[16,2,2,64]{3,2,1,0:T(2,128)(2,1)} custom-call(bf16[8,4,4,128]{3,2,1,0:T(4,128)(2,1)} %v_ref.1, bf16[3,3,3,16,256]{4,3,2,1,0:T(8,128)(2,1)} %bitcast.2, bf16[1,16]{1,0:T(2,128)(2,1)} %bitcast.3), custom_call_target="tpu_custom_call" | custom-call | tf_op jit(solution)/shard_map/pallas_call | solution.py:195
  27.5 1.3 %copy.5 = bf16[16,2,2,64]{3,2,1,0:T(2,128)(2,1)} copy(bf16[16,2,2,64]{3,2,1,0:T(2,128)(2,1)} %shard_map.37) | data formatting | bytes 16384

commit v14 on v13

--- a/solution.py
+++ b/solution.py
@@ -11,9 +11,9 @@
 MESH = pl.DeviceIdType.MESH
 
 
-def gather_kernel(n, slabs, v_ref, w_ref, b_ref, o_ref, acc_ref, part_ref, out_ref, x_ref, send_buf,
+def gather_kernel(n, slabs, v_ref, w_hbm, b_ref, o_ref, acc_ref, part_ref, out_ref, x_ref, send_buf,
                   recv_buf, local_sem, send_sem, fwd_sem, relay_sem, recv_sem,
-                  part_send, part_recv, half_recv, send2_sem):
+                  part_send, part_recv, half_recv, send2_sem, w_ref, w_sem, wmat):
     depth, height, across = v_ref.shape[1:]
     for z in range(depth):
         for y in range(height):
@@ -47,6 +47,14 @@
     barrier = pltpu.get_barrier_semaphore()
     for peer in [sib] + peers:
         pl.semaphore_signal(barrier, inc=1, device_id=(peer, sp), device_id_type=MESH)
+    w_copy = pltpu.make_async_copy(w_hbm, w_ref, w_sem.at[0])
+    w_copy.start()
+    w_copy.wait()
+    wmat[...] = jnp.concatenate(
+        [jnp.concatenate([w_ref[a, b, c] for c in range(3)], axis=1)
+         for a in range(3) for b in range(3)],
+        axis=0,
+    )
     has_lo = sp > 0
     has_hi = sp < slabs - 1
 
@@ -127,11 +135,8 @@
         left = jnp.where(x == 0, zero, pltpu.roll(g, 1, 1))
         right = jnp.where(x == across - 1, zero, pltpu.roll(g, plane - 1, 1))
         stacked = jnp.concatenate([left, g, right], axis=0)
-        weights = jnp.concatenate(
-            [jnp.concatenate([w_ref[a, b, c] for c in range(3)], axis=1) for b in range(3)],
-            axis=0,
-        )
-        q = jnp.dot(weights, stacked, preferred_element_type=jnp.float32)
+        rows3 = 3 * w_ref.shape[3]
+        q = jnp.dot(wmat[a * rows3:(a + 1) * rows3], stacked, preferred_element_type=jnp.float32)
         tiles = []
         for y in range(height):
             total = None
@@ -159,7 +164,7 @@
     def _():
         down.start()
 
-    acc_ref[...] = interior_conv(out_ref, w_ref, plane=plane, row=across, depth=depth)
+    acc_ref[...] = interior_conv(out_ref, wmat, w_ref.shape[3], plane=plane, row=across, depth=depth)
     for c in sends + forwards + relays:
         c.wait_send()
 
@@ -195,7 +200,11 @@
     return pl.pallas_call(
         functools.partial(gather_kernel, n, slabs),
         out_shape=jax.ShapeDtypeStruct((filters, depth // 2, height // 2, across // 2), jnp.bfloat16),
-        in_specs=[pl.BlockSpec(memory_space=pltpu.VMEM)] * 3,
+        in_specs=[
+            pl.BlockSpec(memory_space=pltpu.VMEM),
+            pl.BlockSpec(memory_space=pl.ANY),
+            pl.BlockSpec(memory_space=pltpu.VMEM),
+        ],
         out_specs=pl.BlockSpec(memory_space=pltpu.VMEM),
         scratch_shapes=[
             pltpu.VMEM((filters, cols), jnp.float32),
@@ -213,12 +222,15 @@
             pltpu.SemaphoreType.DMA((2,)),
             pltpu.SemaphoreType.DMA((n,)),
             pltpu.SemaphoreType.DMA((chips,)),
+            pltpu.VMEM(weights.shape, weights.dtype),
+            pltpu.SemaphoreType.DMA((1,)),
+            pltpu.VMEM((9 * filters, 3 * weights.shape[4]), weights.dtype),
         ],
         compiler_params=pltpu.CompilerParams(collective_id=0, has_side_effects=True),
     )(block, weights, bias)
 
 
-def interior_conv(g_ref, w_ref, *, plane, row, depth):
+def interior_conv(g_ref, wmat, filters, *, plane, row, depth):
     g = g_ref[...]
     cols = g.shape[1]
     heights = plane // row
@@ -227,13 +239,7 @@
     left = jnp.where(x == 0, zero, pltpu.roll(g, 1, 1))
     right = jnp.where(x == row - 1, zero, pltpu.roll(g, cols - 1, 1))
     stacked = jnp.concatenate([left, g, right], axis=0)
-    weights = jnp.concatenate(
-        [jnp.concatenate([w_ref[a, b, c] for c in range(3)], axis=1)
-         for a in range(3) for b in range(3)],
-        axis=0,
-    )
-    filters = w_ref.shape[3]
-    q = jnp.dot(weights, stacked, preferred_element_type=jnp.float32)
+    q = jnp.dot(wmat[...], stacked, preferred_element_type=jnp.float32)
 
     def tap_row(a, b, p, y):
         if not 0 <= y < heights:

time: 29.3 us -> 29.2 us (level)
  no operation moved by 1% of the time
where the time goes in v14:
time: 29.2 us; the launch traced here: 28.7 us
  Pallas kernels  27.4 us (94%)
  local copies, waits for them, and re-layouts  1.34 us (5%)
    pallas_call x1, Pallas kernels, gather_filt(): pl.pallas_call(functools.partial(gather_kernel, n, slabs), out_shape=jax....  27.4 us
    unnamed x1, local copies, waits for them, and re-layouts  1.34 us

profile of v14, /device:TPU:7, one launch (start us, length us, event | category | flops | bytes accessed | tf_op | source)
XLA Modules:
  0.0 28.7 jit_solution(13817413789916153106)
XLA Ops:
  0.0 27.4 %shard_map.37 = bf16[16,2,2,64]{3,2,1,0:T(2,128)(2,1)} custom-call(bf16[8,4,4,128]{3,2,1,0:T(4,128)(2,1)} %v_ref.1, bf16[3,3,3,16,256]{4,3,2,1,0:T(8,128)(2,1)} %bitcast.2, bf16[1,16]{1,0:T(2,128)(2,1)} %bitcast.3), custom_call_target="tpu_custom_call" | custom-call | tf_op jit(solution)/shard_map/pallas_call | solution.py:200
  27.4 1.3 %copy.5 = bf16[16,2,2,64]{3,2,1,0:T(2,128)(2,1)} copy(bf16[16,2,2,64]{3,2,1,0:T(2,128)(2,1)} %shard_map.37) | data formatting | bytes 16384
